TPU v7x, 256 devices: a whole 4x4x8 slice. The times are simulated.
256 devices in a mesh: win: 64 (over y, x, z_lo), row: 4 (over z_hi, core).
Axes of the slice: x: 4, y: 4, z: 8 (z_hi: 2, z_lo: 4; z = z_hi * 4 + z_lo), core: 2. Of those that a mesh axis runs over, the one named last changes fastest.
Arguments:
- downgoing: float32 [64, 3072, 3072], P('win', 'row'), may hold values from -64 to 64
- upgoing: float32 [64, 64, 3072], P('win'), may hold values from -6 to 6
Outputs:
- filters: float32 [256, 2, 64, 3072], P('win', None, None, 'row')
All inputs are finite; a program needn't handle non-finite values.
Results may differ from a plain program's by a relative error of at most 0.00016.
Values sent between devices are 32-bit elements; how exact they have to be, the bound alone decides.
No kernel may reach another device: no remote copies, remote signals or barrier semaphores. Data moves between devices by JAX's collectives and lax.ppermute only.
A program may use at most 128 MiB of HBM per device.

v0:
```python
import math

import jax
import jax.numpy as jnp
import numpy as np
from jax import lax
from jax.experimental import pallas as pl
from jax.experimental.pallas import tpu as pltpu
from jax.sharding import PartitionSpec as P

NCH = 3072
NT = 3072
NVS = 64
NWT = 64
NF = 256
DAMPING = 0.5
QUARTER = NT // 4
LANES = 128
CH_TILE = 256
BINS = 4
ROWS_D = 2 * BINS * 6
ROWS = ROWS_D + BINS
F32 = jnp.float32
BF16 = jnp.bfloat16


def split_table(table):
    high = table.astype(BF16)
    low = (table - high.astype(np.float64)).astype(BF16)
    return np.concatenate([high, low], axis=0)


def dft_tables():
    t = np.arange(QUARTER, dtype=np.int64)
    owners = np.arange(NWT, dtype=np.int64)
    scale = 1.0 / math.sqrt(NT)

    def trig(f):
        k = 4 * owners + 1 + f
        angle = (k[:, None] * t[None, :] % NT).astype(np.float64) * (2.0 * math.pi / NT)
        return np.cos(angle) * scale, np.sin(angle) * scale

    odd = []
    for f, sign in ((0, 1.0), (2, -1.0)):
        cos, sin = trig(f)
        odd.append(np.concatenate([cos, -sign * sin], axis=1))
        odd.append(np.concatenate([-sin, -sign * cos], axis=1))
    even = []
    for f in (1, 3):
        cos, sin = trig(f)
        even.append(split_table(np.concatenate([cos, -sin], axis=0)))
    return split_table(np.concatenate(odd, axis=0)), even[0], even[1]


def split(x):
    high = x.astype(BF16)
    return high, (x - high.astype(F32)).astype(BF16)


def dot_nt(a, b):
    return lax.dot_general(a, b, (((1,), (1,)), ((), ())), preferred_element_type=F32)


def dot_nn(a, b):
    return lax.dot_general(a, b, (((1,), (0,)), ((), ())), preferred_element_type=F32)


def table_dot(table_ref, y):
    half = table_ref.shape[0] // 2
    high, low = split(y)
    both = dot_nt(table_ref[...], high)
    return both[:half] + both[half:] + dot_nt(table_ref[pl.ds(0, half), :], low)


def dft_kernel(x_ref, up_ref, todd_ref, t1_ref, t3_ref, o_ref):
    step = pl.program_id(0)

    def spectra(read):
        x0, x1, x2, x3 = (read(q) for q in range(4))
        sum0, sum1, dif0, dif1 = x0 + x2, x1 + x3, x0 - x2, x1 - x3
        odd = table_dot(todd_ref, jnp.concatenate([dif0, dif1], axis=1))
        even1 = table_dot(t1_ref, sum0 - sum1)
        even3 = table_dot(t3_ref, sum0 + sum1)
        return (
            (odd[0:64], odd[64:128]),
            (even1[0:64], even1[64:128]),
            (odd[128:192], odd[192:256]),
            (even3[0:64], even3[64:128]),
        )

    spec = spectra(lambda q: x_ref[:, pl.ds(q * QUARTER, QUARTER)])
    for f in range(BINS):
        for ri in range(2):
            for j in range(CH_TILE // LANES):
                row = (f * 2 + ri) * 6 + step * (CH_TILE // LANES) + j
                o_ref[pl.ds(row, NWT, stride=ROWS), :] = spec[f][ri][:, j * LANES : (j + 1) * LANES]

    @pl.when(step == pl.num_programs(0) - 1)
    def _():
        def read(q):
            part = up_ref[:, pl.ds(q * QUARTER, QUARTER)]
            return jnp.concatenate([part, part], axis=0)

        spec_up = spectra(read)
        left = lax.broadcasted_iota(jnp.int32, (NWT, LANES), 1) < 64
        for f in range(BINS):
            o_ref[pl.ds(ROWS_D + f, NWT, stride=ROWS), :] = jnp.where(left, spec_up[f][0], spec_up[f][1])


def dft(x, up):
    todd, t1, t3 = dft_tables()
    steps = x.shape[0] // CH_TILE

    def whole(a):
        return pl.BlockSpec(a.shape, lambda i: (0, 0), pipeline_mode=pl.Buffered(1))

    return pl.pallas_call(
        dft_kernel,
        out_shape=jax.ShapeDtypeStruct((NWT * ROWS, LANES), F32),
        grid=(steps,),
        in_specs=[
            pl.BlockSpec((CH_TILE, NT), lambda i: (i, 0)),
            whole(up),
            whole(todd),
            whole(t1),
            whole(t3),
        ],
        out_specs=pl.BlockSpec((NWT * ROWS, LANES), lambda i: (0, 0)),
        compiler_params=pltpu.CompilerParams(vmem_limit_bytes=50 << 20),
        cost_estimate=pl.CostEstimate(flops=3 * 10**9, bytes_accessed=15 * 10**6, transcendentals=0),
        name="dft",
    )(x, up, jnp.asarray(todd), jnp.asarray(t1), jnp.asarray(t3))


def bin_rows(r_ref, f, ri):
    return jnp.concatenate(
        [r_ref[pl.ds((f * 2 + ri) * 6 + ct, NWT, stride=ROWS), :] for ct in range(6)], axis=1
    )


def gram_kernel(r_ref, g_ref):
    lane = lax.broadcasted_iota(jnp.int32, (NWT, LANES), 1)
    row = lax.broadcasted_iota(jnp.int32, (NWT, LANES), 0)
    upper = row <= lane % 64
    left = lane < 64
    packed = []
    for f in range(BINS):
        re_h, re_l = split(bin_rows(r_ref, f, 0))
        im_h, im_l = split(bin_rows(r_ref, f, 1))
        lhs_h = jnp.concatenate([re_h, im_h], axis=1)
        lhs_l = jnp.concatenate([re_l, im_l], axis=1)
        rhs_h = jnp.concatenate([lhs_h, jnp.concatenate([im_h, -re_h], axis=1)], axis=0)
        rhs_l = jnp.concatenate([lhs_l, jnp.concatenate([im_l, -re_l], axis=1)], axis=0)
        both = dot_nt(lhs_h, rhs_h) + dot_nt(lhs_h, rhs_l) + dot_nt(lhs_l, rhs_h)
        swapped = pltpu.roll(both, 64, 1)
        packed.append(jnp.where(upper == left, both, swapped))
    for pair in range(BINS // 2):
        g_ref[pair] = jnp.where(left, packed[2 * pair], packed[2 * pair + 1])


def gram(recv):
    return pl.pallas_call(
        gram_kernel,
        out_shape=jax.ShapeDtypeStruct((BINS // 2, NWT, LANES), F32),
        compiler_params=pltpu.CompilerParams(vmem_limit_bytes=40 << 20),
        cost_estimate=pl.CostEstimate(flops=3 * 10**8, bytes_accessed=2 * 10**6, transcendentals=0),
        name="gram",
    )(recv)


def dot3(a, b_h, b_l):
    a_h, a_l = split(a)
    return dot_nn(a_h, b_h) + dot_nn(a_l, b_h) + dot_nn(a_h, b_l)


def row_dot(a, b):
    return jnp.sum(a * b, axis=1, keepdims=True)


def solve_kernel(r_ref, ga_ref, gb_ref, o_ref):
    lane = lax.broadcasted_iota(jnp.int32, (NWT, LANES), 1)
    row = lax.broadcasted_iota(jnp.int32, (NWT, LANES), 0)
    col = lane % 64
    left = lane < 64
    grams = []
    for pair in range(BINS // 2):
        packed = ga_ref[pair] + gb_ref[pair]
        turned = jnp.concatenate([packed, packed], axis=0).T
        other = pltpu.roll(packed, 64, 1)
        for half in range(2):
            here = jnp.where(left == (half == 0), packed, other)
            there = turned[half * 64 : half * 64 + 64]
            real = jnp.where(row <= col, here, there)
            imag = jnp.where(row > col, here, jnp.where(row == col, 0.0, -there))
            top = jnp.where(left, real, imag)
            bottom = jnp.where(left, -imag, real)
            grams.append(split(jnp.concatenate([top, bottom], axis=0)))
    starts = []
    for f in range(BINS):
        up = r_ref[pl.ds(ROWS_D + f, NWT, stride=ROWS), :]
        turned = jnp.concatenate([up, up], axis=0).T
        starts.append(jnp.where(left, turned[:64], turned[64:]) * (1.0 / math.sqrt(NCH)))

    def times_gram(ys):
        return [dot3(y, *g) for y, g in zip(ys, grams)]

    res = starts
    res_g = times_gram(res)
    res_gg = times_gram(res_g)
    for f in range(BINS):
        dir0, dir0_g, dir0_gg = res[f], res_g[f], res_gg[f]
        norm0 = row_dot(dir0, dir0_g)
        img = dir0_g * (1.0 / NCH) + DAMPING * dir0
        img_g = dir0_gg * (1.0 / NCH) + DAMPING * dir0_g
        step0 = norm0 / row_dot(dir0_g, img)
        res1 = dir0 - step0 * img
        res1_g = dir0_g - step0 * img_g
        norm1 = row_dot(res1, res1_g)
        ratio = norm1 / norm0
        dir1 = res1 + ratio * dir0
        dir1_g = res1_g + ratio * dir0_g
        img1 = dir1_g * (1.0 / NCH) + DAMPING * dir1
        step1 = norm1 / row_dot(dir1_g, img1)
        filt = (step0 * dir0 + step1 * dir1) * math.sqrt(NCH / NWT)
        turned = pltpu.roll(filt, 64, 1)
        lhs_h, lhs_l = split(jnp.concatenate([filt, jnp.where(left, turned, -turned)], axis=0))
        rhs_h, rhs_l = split(jnp.concatenate([bin_rows(r_ref, f, 0), bin_rows(r_ref, f, 1)], axis=0))
        out = dot_nn(lhs_h, rhs_h) + dot_nn(lhs_l, rhs_h) + dot_nn(lhs_h, rhs_l)
        o_ref[f, 0] = out[:64]
        o_ref[f, 1] = out[64:]


def solve(recv, gram_a, gram_b, channels):
    return pl.pallas_call(
        solve_kernel,
        out_shape=jax.ShapeDtypeStruct((BINS, 2, NVS, channels), F32),
        compiler_params=pltpu.CompilerParams(vmem_limit_bytes=40 << 20),
        cost_estimate=pl.CostEstimate(flops=3 * 10**8, bytes_accessed=4 * 10**6, transcendentals=0),
        name="solve",
    )(recv, gram_a, gram_b)


CORE_PAIRS = [(0, 1), (1, 0), (2, 3), (3, 2)]
FAR_PAIRS = [(0, 2), (2, 0), (1, 3), (3, 1)]


def body(downgoing, upgoing):
    channels = downgoing.shape[1]
    sent = dft(downgoing[0], upgoing[0])
    sent = sent.reshape(NWT, ROWS // 4, 4, LANES)
    recv = lax.all_to_all(sent, "win", split_axis=0, concat_axis=0, tiled=True)
    recv = recv.reshape(NWT * ROWS, LANES)
    part = gram(recv)
    chip = part + lax.ppermute(part, "row", CORE_PAIRS)
    far = lax.ppermute(chip, "row", FAR_PAIRS)
    return solve(recv, chip, far, channels)


def solution(mesh):
    in_specs = (P("win", "row", None), P("win", None, None))
    out_specs = P("win", None, None, "row")
    return jax.shard_map(body, mesh=mesh, in_specs=in_specs, out_specs=out_specs, check_vma=False)
```

profile of v0, /device:TPU:1, one launch (start us, length us, event | category | flops | bytes accessed | tf_op | source)
XLA Modules:
  0.0 82.6 jit_solution(14741001228952613971)
XLA Ops:
  0.0 0.0 copy-start
  0.0 1.4 %copy-done = bf16[512,1536]{1,0:T(8,128)(2,1)S(1)} copy-done((bf16[512,1536]{1,0:T(8,128)(2,1)S(1)}, bf16[512,1536]{1,0:T(8,128)(2,1)}, u32[]{:S(2)}) %copy-start) | copy-done | bytes 1572888
  1.4 0.0 copy-start.1
  1.4 1.1 %copy-done.1 = f32[1,64,3072]{2,1,0:T(8,128)S(1)} copy-done((f32[1,64,3072]{2,1,0:T(8,128)S(1)}, f32[1,64,3072]{2,1,0:T(8,128)}, u32[]{:S(2)}) %copy-start.1) | copy-done | bytes 786456
  2.5 0.0 copy-start.2
  2.5 1.0 %copy-done.2 = bf16[256,768]{1,0:T(8,128)(2,1)S(1)} copy-done((bf16[256,768]{1,0:T(8,128)(2,1)S(1)}, bf16[256,768]{1,0:T(8,128)(2,1)}, u32[]{:S(2)}) %copy-start.2) | copy-done | bytes 393240
  3.5 0.0 copy-start.3
  3.5 1.0 %copy-done.3 = bf16[256,768]{1,0:T(8,128)(2,1)S(1)} copy-done((bf16[256,768]{1,0:T(8,128)(2,1)S(1)}, bf16[256,768]{1,0:T(8,128)(2,1)}, u32[]{:S(2)}) %copy-start.3) | copy-done | bytes 393240
  4.5 8.6 %dft.1 = f32[3328,128]{1,0:T(8,128)} custom-call(f32[768,3072]{1,0:T(8,128)} %bitcast.7, f32[64,3072]{1,0:T(8,128)S(1)} %bitcast.6, bf16[512,1536]{1,0:T(8,128)(2,1)S(1)} %copy-done, bf16[256,768]{1,0:T(8,128)(2,1)S(1)} %copy-done.3, bf16[256,768]{1,0:T(8,128)(2,1)S(1)} %copy-done.2), custom_call_target="tpu_custom_call" | custom-call | flops 3000000000 | bytes 15000000 | tf_op jit(solution)/shard_map/dft/pallas_call | solution.py:117
  13.2 54.6 %all_to_all.5 = f32[64,13,4,128]{3,2,1,0:T(4,128)S(1)} all-to-all(f32[64,13,4,128]{3,2,1,0:T(4,128)} %bitcast.8), channel_id=1, replica_groups=mesh['win'=64,'row'=4] {'win'}, dimensions={0} | all-to-all | bytes 3407872 | tf_op jit(solution)/shard_map/all_to_all | solution.py:251
  67.8 1.8 %gram.1 = f32[2,64,128]{2,1,0:T(8,128)S(1)} custom-call(f32[3328,128]{1,0:T(8,128)S(1)} %bitcast.4), custom_call_target="tpu_custom_call" | custom-call | flops 300000000 | bytes 2000000 | tf_op jit(solution)/shard_map/gram/pallas_call | solution.py:162
  69.6 2.4 %collective-permute-start = (f32[2,64,128]{2,1,0:T(8,128)S(1)}, f32[2,64,128]{2,1,0:T(8,128)S(1)}, u32[]{:S(2)}, u32[]{:S(2)}) collective-permute-start(f32[2,64,128]{2,1,0:T(8,128)S(1)} %gram.1), channel_id=1, source_target_pairs={{0,1},{1,0},{2,3},{3,2},{4,5},{5,4},{6,7},{7,6},{8,9},{9,8},{10,11... | collective-permute-start | bytes 196616 | tf_op jit(solution)/shard_map/ppermute | solution.py:254
  72.0 0.9 %collective-permute-done = f32[2,64,128]{2,1,0:T(8,128)S(1)} collective-permute-done((f32[2,64,128]{2,1,0:T(8,128)S(1)}, f32[2,64,128]{2,1,0:T(8,128)S(1)}, u32[]{:S(2)}, u32[]{:S(2)}) %collective-permute-start) | collective-permute-done | bytes 65568 | tf_op jit(solution)/shard_map/ppermute | solution.py:254
  72.9 4.3 %collective-permute-start.1 = (f32[2,64,128]{2,1,0:T(8,128)S(1)}, f32[2,64,128]{2,1,0:T(8,128)S(1)}, u32[]{:S(2)}, u32[]{:S(2)}) collective-permute-start(f32[2,64,128]{2,1,0:T(8,128)S(1)} %add.3.ga_ref), channel_id=1, source_target_pairs={{0,2},{2,0},{1,3},{3,1},{4,6},{6,4},{5,7},{7,5},{8,10},{10,8},{9,1... | collective-permute-start | bytes 196616 | tf_op jit(solution)/shard_map/ppermute | solution.py:255
  77.2 2.8 %collective-permute-done.1.gb_ref = f32[2,64,128]{2,1,0:T(8,128)S(1)} collective-permute-done((f32[2,64,128]{2,1,0:T(8,128)S(1)}, f32[2,64,128]{2,1,0:T(8,128)S(1)}, u32[]{:S(2)}, u32[]{:S(2)}) %collective-permute-start.1) | collective-permute-done | bytes 65568 | tf_op jit(solution)/shard_map/ppermute | solution.py:255
  80.1 2.6 %solve.1 = f32[4,2,64,768]{3,2,1,0:T(8,128)} custom-call(f32[3328,128]{1,0:T(8,128)S(1)} %bitcast.5, f32[2,64,128]{2,1,0:T(8,128)S(1)} %add.3.ga_ref, f32[2,64,128]{2,1,0:T(8,128)S(1)} %collective-permute-done.1.gb_ref), custom_call_target="tpu_custom_call" | custom-call | flops 300000000 | bytes 4000000 | tf_op jit(solution)/shard_map/solve/pallas_call | solution.py:234
  (1 shorter events, 0.0 us)
Async XLA Ops:
  0.0 1.4 %copy-start = (bf16[512,1536]{1,0:T(8,128)(2,1)S(1)}, bf16[512,1536]{1,0:T(8,128)(2,1)}, u32[]{:S(2)}) copy-start(bf16[512,1536]{1,0:T(8,128)(2,1)} %constant.6.clone.todd_ref) | copy-start | bytes 4718596
  1.4 1.1 %copy-start.1 = (f32[1,64,3072]{2,1,0:T(8,128)S(1)}, f32[1,64,3072]{2,1,0:T(8,128)}, u32[]{:S(2)}) copy-start(f32[1,64,3072]{2,1,0:T(8,128)} %param.6) | copy-start | bytes 2359300
  2.5 1.0 %copy-start.2 = (bf16[256,768]{1,0:T(8,128)(2,1)S(1)}, bf16[256,768]{1,0:T(8,128)(2,1)}, u32[]{:S(2)}) copy-start(bf16[256,768]{1,0:T(8,128)(2,1)} %constant.8.clone.t3_ref) | copy-start | bytes 1179652
  3.5 1.0 %copy-start.3 = (bf16[256,768]{1,0:T(8,128)(2,1)S(1)}, bf16[256,768]{1,0:T(8,128)(2,1)}, u32[]{:S(2)}) copy-start(bf16[256,768]{1,0:T(8,128)(2,1)} %constant.7.clone.t1_ref) | copy-start | bytes 1179652
  69.6 3.3 %collective-permute-start = (f32[2,64,128]{2,1,0:T(8,128)S(1)}, f32[2,64,128]{2,1,0:T(8,128)S(1)}, u32[]{:S(2)}, u32[]{:S(2)}) collective-permute-start(f32[2,64,128]{2,1,0:T(8,128)S(1)} %gram.1), channel_id=1, source_target_pairs={{0,1},{1,0},{2,3},{3,2},{4,5},{5,4},{6,7},{7,6},{8,9},{9,8},{10,11... | collective-permute-start | bytes 196616 | tf_op jit(solution)/shard_map/ppermute | solution.py:254
  72.9 7.1 %collective-permute-start.1 = (f32[2,64,128]{2,1,0:T(8,128)S(1)}, f32[2,64,128]{2,1,0:T(8,128)S(1)}, u32[]{:S(2)}, u32[]{:S(2)}) collective-permute-start(f32[2,64,128]{2,1,0:T(8,128)S(1)} %add.3.ga_ref), channel_id=1, source_target_pairs={{0,2},{2,0},{1,3},{3,1},{4,6},{6,4},{5,7},{7,5},{8,10},{10,8},{9,1... | collective-permute-start | bytes 196616 | tf_op jit(solution)/shard_map/ppermute | solution.py:255
where the time goes:
time: 83.5 us; the launch traced here: 82.6 us
  blocking collectives  54.6 us (65%)
  Pallas kernels  13 us (16%)
  starting transfers between devices  6.71 us (8%)
  local copies, waits for them, and re-layouts  4.53 us (5%)
  waiting for transfers between devices  3.71 us (4%)
    all_to_all x1, blocking collectives, body(): recv = lax.all_to_all(sent, 'win', split_axis=0, concat_axis=0, tiled=True)  54.6 us
    pallas_call x1, Pallas kernels, dft(): pl.pallas_call(dft_kernel, out_shape=jax.ShapeDtypeStruct((NWT * ROWS, LA...  8.65 us
    unnamed x8, local copies, waits for them, and re-layouts  4.53 us
    ppermute x1, starting transfers between devices, body(): far = lax.ppermute(chip, 'row', FAR_PAIRS)  4.3 us
    ppermute x1, waiting for transfers between devices, body(): far = lax.ppermute(chip, 'row', FAR_PAIRS)  2.81 us
    pallas_call x1, Pallas kernels, solve(): pl.pallas_call(solve_kernel, out_shape=jax.ShapeDtypeStruct((BINS, 2, NVS...  2.59 us
    ppermute x1, starting transfers between devices, body(): chip = part + lax.ppermute(part, 'row', CORE_PAIRS)  2.41 us
    pallas_call x1, Pallas kernels, gram(): pl.pallas_call(gram_kernel, out_shape=jax.ShapeDtypeStruct((BINS // 2, NW...  1.79 us
  transfers between devices with their start and end apart: 2, of which 2 were waited for; matrix products, arithmetic and copies ran while one was open for 0% of the time, Pallas kernels for 0%

commit v1 on v0

v1 whole, which is shorter than its diff:
```python
import math

import jax
import jax.numpy as jnp
import numpy as np
from jax import lax
from jax.experimental import pallas as pl
from jax.experimental.pallas import tpu as pltpu
from jax.sharding import PartitionSpec as P

NCH = 3072
NT = 3072
NVS = 64
NWT = 64
NF = 256
DAMPING = 0.5
QUARTER = NT // 4
LANES = 128
CH_TILE = 256
FOLD_ROWS = 16
VMEM_LIMIT = 60 << 20
BINS = 4
ROWS_D = 2 * BINS * 6
ROWS = ROWS_D + BINS
F32 = jnp.float32
BF16 = jnp.bfloat16


def split_table(table):
    high = table.astype(BF16)
    low = (table - high.astype(np.float64)).astype(BF16)
    return np.concatenate([high, low], axis=0)


def dft_tables():
    t = np.arange(QUARTER, dtype=np.int64)
    owners = np.arange(NWT, dtype=np.int64)
    scale = 1.0 / math.sqrt(NT)

    def trig(f):
        k = 4 * owners + 1 + f
        angle = (k[:, None] * t[None, :] % NT).astype(np.float64) * (2.0 * math.pi / NT)
        return np.cos(angle) * scale, np.sin(angle) * scale

    odd = []
    for f, sign in ((0, 1.0), (2, -1.0)):
        cos, sin = trig(f)
        odd.append(np.concatenate([cos, -sign * sin], axis=1))
        odd.append(np.concatenate([-sin, -sign * cos], axis=1))
    even = []
    for f in (1, 3):
        cos, sin = trig(f)
        even.append(split_table(np.concatenate([cos, -sin], axis=0)))
    return np.concatenate([split_table(np.concatenate(odd, axis=0)), np.concatenate(even, axis=0)], axis=1)


def split(x):
    high = x.astype(BF16)
    return high, (x - high.astype(F32)).astype(BF16)


def dot_nt(a, b):
    return lax.dot_general(a, b, (((1,), (1,)), ((), ())), preferred_element_type=F32)


def dot_nn(a, b):
    return lax.dot_general(a, b, (((1,), (0,)), ((), ())), preferred_element_type=F32)


def table_dot(table, high, low):
    half = table.shape[0] // 2
    both = dot_nt(table, high)
    return both[:half] + both[half:] + dot_nt(table[:half], low)


def dft_kernel(x_hbm, up_hbm, table_hbm, o_ref, x_ref, table_ref, high_ref, low_ref, x_sem, up_sem, table_sem):
    channels = x_hbm.shape[0]
    tiles = channels // CH_TILE

    def x_copy(i):
        rows = pl.ds(pl.multiple_of(i * CH_TILE, CH_TILE), CH_TILE)
        return pltpu.make_async_copy(x_hbm.at[rows], x_ref.at[rows], x_sem.at[i])

    up_copy = pltpu.make_async_copy(up_hbm, x_ref.at[pl.ds(channels, NVS)], up_sem)
    table_copy = pltpu.make_async_copy(table_hbm, table_ref, table_sem)
    x_copy(0).start()
    table_copy.start()
    x_copy(1).start()

    def fold(first, count):
        for r in range(0, count, FOLD_ROWS):
            x0, x1, x2, x3 = (
                x_ref[pl.ds(first + r, FOLD_ROWS), pl.ds(q * QUARTER, QUARTER)] for q in range(4)
            )
            sum0, sum1 = x0 + x2, x1 + x3
            for k, y in enumerate((x0 - x2, x1 - x3, sum0 - sum1, sum0 + sum1)):
                high, low = split(y)
                high_ref[pl.ds(r, FOLD_ROWS), pl.ds(k * QUARTER, QUARTER)] = high
                low_ref[pl.ds(r, FOLD_ROWS), pl.ds(k * QUARTER, QUARTER)] = low

    def spectra(count):
        def part(rows, table_col, col, size):
            table = table_ref[pl.ds(*rows), pl.ds(table_col, size)]
            cut = (pl.ds(0, count), pl.ds(col, size))
            return table_dot(table, high_ref[cut], low_ref[cut])

        odd = part((0, 512), 0, 0, 2 * QUARTER)
        even1 = part((0, 256), 2 * QUARTER, 2 * QUARTER, QUARTER)
        even3 = part((256, 256), 2 * QUARTER, 3 * QUARTER, QUARTER)
        return (
            (odd[0:64], odd[64:128]),
            (even1[0:64], even1[64:128]),
            (odd[128:192], odd[192:256]),
            (even3[0:64], even3[64:128]),
        )

    @pl.loop(0, tiles)
    def _(i):
        x_copy(i).wait()

        @pl.when(i + 2 < tiles)
        def _():
            x_copy(i + 2).start()

        @pl.when(i + 2 == tiles)
        def _():
            up_copy.start()

        fold(pl.multiple_of(i * CH_TILE, CH_TILE), CH_TILE)

        @pl.when(i == 0)
        def _():
            table_copy.wait()

        spec = spectra(CH_TILE)
        for f in range(BINS):
            for ri in range(2):
                for j in range(CH_TILE // LANES):
                    row = (f * 2 + ri) * 6 + i * (CH_TILE // LANES) + j
                    o_ref[pl.ds(row, NWT, stride=ROWS), :] = spec[f][ri][:, j * LANES : (j + 1) * LANES]

    up_copy.wait()
    fold(channels, NVS)
    for ref in (high_ref, low_ref):
        ref[pl.ds(NVS, NVS)] = ref[pl.ds(0, NVS)]
    spec_up = spectra(2 * NVS)
    left = lax.broadcasted_iota(jnp.int32, (NWT, LANES), 1) < 64
    for f in range(BINS):
        o_ref[pl.ds(ROWS_D + f, NWT, stride=ROWS), :] = jnp.where(left, spec_up[f][0], spec_up[f][1])


def dft(x, up):
    table = dft_tables()
    channels = x.shape[0]
    in_hbm = pl.BlockSpec(memory_space=pltpu.HBM)
    return pl.pallas_call(
        dft_kernel,
        out_shape=pltpu.VMEM((NWT * ROWS, LANES), F32),
        in_specs=[in_hbm, in_hbm, in_hbm],
        scratch_shapes=[
            pltpu.VMEM((channels + NVS, NT), F32),
            pltpu.VMEM(table.shape, BF16),
            pltpu.VMEM((CH_TILE, NT), BF16),
            pltpu.VMEM((CH_TILE, NT), BF16),
            pltpu.SemaphoreType.DMA((channels // CH_TILE,)),
            pltpu.SemaphoreType.DMA,
            pltpu.SemaphoreType.DMA,
        ],
        compiler_params=pltpu.CompilerParams(vmem_limit_bytes=VMEM_LIMIT),
        cost_estimate=pl.CostEstimate(flops=3 * 10**9, bytes_accessed=15 * 10**6, transcendentals=0),
        name="dft",
    )(x, up, jnp.asarray(table))


def bin_rows(r_ref, f, ri):
    return jnp.concatenate(
        [r_ref[pl.ds((f * 2 + ri) * 6 + ct, NWT, stride=ROWS), :] for ct in range(6)], axis=1
    )


def bin_matrix(r_ref, f):
    return split(jnp.concatenate([bin_rows(r_ref, f, 0), bin_rows(r_ref, f, 1)], axis=0))


def gram_kernel(r_ref, g_ref):
    lane = lax.broadcasted_iota(jnp.int32, (NWT, LANES), 1)
    row = lax.broadcasted_iota(jnp.int32, (NWT, LANES), 0)
    upper = row <= lane % 64
    left = lane < 64
    packed = []
    for f in range(BINS):
        high, low = bin_matrix(r_ref, f)
        both = dot_nt(jnp.concatenate([high, low], axis=0), high)
        cross = both[LANES:]
        total = both[:LANES] + cross + cross.T
        below = pltpu.roll(total[64:], 64, 1)
        both = total[:64] + jnp.where(left, below, -below)
        swapped = pltpu.roll(both, 64, 1)
        packed.append(jnp.where(upper == left, both, swapped))
    for pair in range(BINS // 2):
        g_ref[pair] = jnp.where(left, packed[2 * pair], packed[2 * pair + 1])


def gram(recv):
    return pl.pallas_call(
        gram_kernel,
        out_shape=jax.ShapeDtypeStruct((BINS // 2, NWT, LANES), F32),
        compiler_params=pltpu.CompilerParams(vmem_limit_bytes=40 << 20),
        cost_estimate=pl.CostEstimate(flops=3 * 10**8, bytes_accessed=2 * 10**6, transcendentals=0),
        name="gram",
    )(recv)


def prep_kernel(r_ref, high_ref, low_ref, start_ref):
    left = lax.broadcasted_iota(jnp.int32, (NWT, LANES), 1) < 64
    for f in range(BINS):
        high_ref[f], low_ref[f] = bin_matrix(r_ref, f)
        up = r_ref[pl.ds(ROWS_D + f, NWT, stride=ROWS), :]
        turned = jnp.concatenate([up, up], axis=0).T
        start_ref[f] = jnp.where(left, turned[:64], turned[64:]) * (1.0 / math.sqrt(NCH))


def prep(recv, channels):
    matrices = pltpu.VMEM((BINS, 2 * NWT, channels), BF16)
    return pl.pallas_call(
        prep_kernel,
        out_shape=(matrices, matrices, pltpu.VMEM((BINS, NVS, LANES), F32)),
        compiler_params=pltpu.CompilerParams(vmem_limit_bytes=40 << 20),
        cost_estimate=pl.CostEstimate(flops=10**7, bytes_accessed=4 * 10**6, transcendentals=0),
        name="prep",
    )(recv)


def dot3(a, b_h, b_l):
    a_h, a_l = split(a)
    return dot_nn(a_h, b_h) + dot_nn(a_l, b_h) + dot_nn(a_h, b_l)


def row_dot(a, b):
    return jnp.sum(a * b, axis=1, keepdims=True)


def solve_kernel(high_ref, low_ref, start_ref, ga_ref, gb_ref, o_ref):
    lane = lax.broadcasted_iota(jnp.int32, (NWT, LANES), 1)
    row = lax.broadcasted_iota(jnp.int32, (NWT, LANES), 0)
    col = lane % 64
    left = lane < 64
    grams = []
    for pair in range(BINS // 2):
        packed = ga_ref[pair] + gb_ref[pair]
        turned = jnp.concatenate([packed, packed], axis=0).T
        other = pltpu.roll(packed, 64, 1)
        for half in range(2):
            here = jnp.where(left == (half == 0), packed, other)
            there = turned[half * 64 : half * 64 + 64]
            real = jnp.where(row <= col, here, there)
            imag = jnp.where(row > col, here, jnp.where(row == col, 0.0, -there))
            top = jnp.where(left, real, imag)
            bottom = jnp.where(left, -imag, real)
            grams.append(split(jnp.concatenate([top, bottom], axis=0)))
    starts = [start_ref[f] for f in range(BINS)]

    def times_gram(ys):
        return [dot3(y, *g) for y, g in zip(ys, grams)]

    res = starts
    res_g = times_gram(res)
    res_gg = times_gram(res_g)
    for f in range(BINS):
        dir0, dir0_g, dir0_gg = res[f], res_g[f], res_gg[f]
        norm0 = row_dot(dir0, dir0_g)
        img = dir0_g * (1.0 / NCH) + DAMPING * dir0
        img_g = dir0_gg * (1.0 / NCH) + DAMPING * dir0_g
        step0 = norm0 / row_dot(dir0_g, img)
        res1 = dir0 - step0 * img
        res1_g = dir0_g - step0 * img_g
        norm1 = row_dot(res1, res1_g)
        ratio = norm1 / norm0
        dir1 = res1 + ratio * dir0
        dir1_g = res1_g + ratio * dir0_g
        img1 = dir1_g * (1.0 / NCH) + DAMPING * dir1
        step1 = norm1 / row_dot(dir1_g, img1)
        filt = (step0 * dir0 + step1 * dir1) * math.sqrt(NCH / NWT)
        turned = pltpu.roll(filt, 64, 1)
        lhs_h, lhs_l = split(jnp.concatenate([filt, jnp.where(left, turned, -turned)], axis=0))
        both = dot_nn(jnp.concatenate([lhs_h, lhs_l], axis=0), high_ref[f])
        out = both[:LANES] + both[LANES:] + dot_nn(lhs_h, low_ref[f])
        o_ref[f, 0] = out[:64]
        o_ref[f, 1] = out[64:]


def solve(prepared, gram_a, gram_b, channels):
    return pl.pallas_call(
        solve_kernel,
        out_shape=jax.ShapeDtypeStruct((BINS, 2, NVS, channels), F32),
        compiler_params=pltpu.CompilerParams(vmem_limit_bytes=40 << 20),
        cost_estimate=pl.CostEstimate(flops=3 * 10**8, bytes_accessed=4 * 10**6, transcendentals=0),
        name="solve",
    )(*prepared, gram_a, gram_b)


CORE_PAIRS = [(0, 1), (1, 0), (2, 3), (3, 2)]
FAR_PAIRS = [(0, 2), (2, 0), (1, 3), (3, 1)]


def body(downgoing, upgoing):
    channels = downgoing.shape[1]
    sent = dft(downgoing[0], upgoing[0])
    sent = sent.reshape(NWT, ROWS // 4, 4, LANES)
    recv = lax.all_to_all(sent, "win", split_axis=0, concat_axis=0, tiled=True)
    recv = recv.reshape(NWT * ROWS, LANES)
    part = gram(recv)
    chip = part + lax.ppermute(part, "row", CORE_PAIRS)
    far = lax.ppermute(chip, "row", FAR_PAIRS)
    return solve(prep(recv, channels), chip, far, channels)


def solution(mesh):
    in_specs = (P("win", "row", None), P("win", None, None))
    out_specs = P("win", None, None, "row")
    return jax.shard_map(body, mesh=mesh, in_specs=in_specs, out_specs=out_specs, check_vma=False)
```

time: 83.5 us -> 77.7 us (0.931)
  local copies, waits for them, and re-layouts: 4.53 us -> 0 us
    unnamed x8 -> x0, local copies, waits for them, and re-layouts: 4.53 us -> none
    pallas_call x1, Pallas kernels: 1.79 us -> 0.82 us  [gram(): pl.pallas_call(gram_kernel, out_shape=jax.ShapeDtypeStruct((BINS // 2, NW...]
    pallas_call x1 -> x2, Pallas kernels: 8.65 us -> 9 us  [the longest x1 8.54 us: dft(): pl.pallas_call(dft_kernel, out_shape=pltpu.VMEM((NWT * ROWS, LANES), F32)...]
  transfers between devices with their start and end apart: 2 -> 2, of which waited for: 2 -> 2; matrix products, arithmetic and copies ran while one was open for 0% -> 0% of each run, Pallas kernels for 0% -> 1%
where the time goes in v1:
time: 77.7 us; the launch traced here: 77.1 us
  blocking collectives  54.4 us (70%)
  Pallas kernels  12.7 us (16%)
  starting transfers between devices  6.73 us (9%)
  waiting for transfers between devices  3.22 us (4%)
    all_to_all x1, blocking collectives, body(): recv = lax.all_to_all(sent, 'win', split_axis=0, concat_axis=0, tiled=True)  54.4 us
    pallas_call x1, Pallas kernels, dft(): pl.pallas_call(dft_kernel, out_shape=pltpu.VMEM((NWT * ROWS, LANES), F32)...  8.54 us
    ppermute x1, starting transfers between devices, body(): far = lax.ppermute(chip, 'row', FAR_PAIRS)  4.32 us
    pallas_call x1, Pallas kernels, solve(): pl.pallas_call(solve_kernel, out_shape=jax.ShapeDtypeStruct((BINS, 2, NVS...  2.87 us
    ppermute x1, starting transfers between devices, body(): chip = part + lax.ppermute(part, 'row', CORE_PAIRS)  2.41 us
    ppermute x1, waiting for transfers between devices, body(): far = lax.ppermute(chip, 'row', FAR_PAIRS)  2.32 us
  transfers between devices with their start and end apart: 2, of which 2 were waited for; matrix products, arithmetic and copies ran while one was open for 0% of the time, Pallas kernels for 1%

profile of v1, /device:TPU:1, one launch (start us, length us, event | category | flops | bytes accessed | tf_op | source)
XLA Modules:
  0.0 77.1 jit_solution(2226473879088775859)
XLA Ops:
  0.0 8.5 %dft.1 = f32[3328,128]{1,0:T(8,128)S(1)} custom-call(f32[768,3072]{1,0:T(8,128)} %bitcast.7, f32[64,3072]{1,0:T(8,128)} %bitcast.8, bf16[512,2304]{1,0:T(8,128)(2,1)} %constant.2.clone.table_hbm), custom_call_target="tpu_custom_call" | custom-call | flops 3000000000 | bytes 15000000 | tf_op jit(solution)/shard_map/dft/pallas_call | solution.py:156
  8.6 54.4 %all_to_all.5 = f32[64,13,4,128]{3,2,1,0:T(4,128)S(1)} all-to-all(f32[64,13,4,128]{3,2,1,0:T(4,128)S(1)} %bitcast.6), channel_id=1, replica_groups=mesh['win'=64,'row'=4] {'win'}, dimensions={0} | all-to-all | bytes 3407872 | tf_op jit(solution)/shard_map/all_to_all | solution.py:310
  63.0 0.8 %gram.1 = f32[2,64,128]{2,1,0:T(8,128)S(1)} custom-call(f32[3328,128]{1,0:T(8,128)S(1)} %bitcast.4), custom_call_target="tpu_custom_call" | custom-call | flops 300000000 | bytes 2000000 | tf_op jit(solution)/shard_map/gram/pallas_call | solution.py:205
  63.8 2.4 %collective-permute-start = (f32[2,64,128]{2,1,0:T(8,128)S(1)}, f32[2,64,128]{2,1,0:T(8,128)S(1)}, u32[]{:S(2)}, u32[]{:S(2)}) collective-permute-start(f32[2,64,128]{2,1,0:T(8,128)S(1)} %gram.1), channel_id=1, source_target_pairs={{0,1},{1,0},{2,3},{3,2},{4,5},{5,4},{6,7},{7,6},{8,9},{9,8},{10,11... | collective-permute-start | bytes 196616 | tf_op jit(solution)/shard_map/ppermute | solution.py:313
  66.2 0.9 %collective-permute-done = f32[2,64,128]{2,1,0:T(8,128)S(1)} collective-permute-done((f32[2,64,128]{2,1,0:T(8,128)S(1)}, f32[2,64,128]{2,1,0:T(8,128)S(1)}, u32[]{:S(2)}, u32[]{:S(2)}) %collective-permute-start) | collective-permute-done | bytes 65568 | tf_op jit(solution)/shard_map/ppermute | solution.py:313
  67.1 4.3 %collective-permute-start.1 = (f32[2,64,128]{2,1,0:T(8,128)S(1)}, f32[2,64,128]{2,1,0:T(8,128)S(1)}, u32[]{:S(2)}, u32[]{:S(2)}) collective-permute-start(f32[2,64,128]{2,1,0:T(8,128)S(1)} %add.3.ga_ref), channel_id=1, source_target_pairs={{0,2},{2,0},{1,3},{3,1},{4,6},{6,4},{5,7},{7,5},{8,10},{10,8},{9,1... | collective-permute-start | bytes 196616 | tf_op jit(solution)/shard_map/ppermute | solution.py:314
  71.4 0.5 prep.1
  71.9 2.3 %collective-permute-done.1.gb_ref = f32[2,64,128]{2,1,0:T(8,128)S(1)} collective-permute-done((f32[2,64,128]{2,1,0:T(8,128)S(1)}, f32[2,64,128]{2,1,0:T(8,128)S(1)}, u32[]{:S(2)}, u32[]{:S(2)}) %collective-permute-start.1) | collective-permute-done | bytes 65568 | tf_op jit(solution)/shard_map/ppermute | solution.py:314
  74.2 2.9 %solve.1 = f32[4,2,64,768]{3,2,1,0:T(8,128)} custom-call(bf16[4,128,768]{2,1,0:T(8,128)(2,1)S(1)} %get-tuple-element.8.high_ref, bf16[4,128,768]{2,1,0:T(8,128)(2,1)S(1)} %get-tuple-element.9.low_ref, f32[4,64,128]{2,1,0:T(8,128)S(1)} %get-tuple-element.10.start_ref, f32[2,64,128]{2,1,0:T(8,128)S(1)} %add.3.ga_ref, ...), custom_call_target="tpu_custom_call" | custom-call | flops 300000000 | bytes 4000000 | tf_op jit(solution)/shard_map/solve/pallas_call | solution.py:293
  (1 shorter events, 0.0 us)
Async XLA Ops:
  63.8 3.3 %collective-permute-start = (f32[2,64,128]{2,1,0:T(8,128)S(1)}, f32[2,64,128]{2,1,0:T(8,128)S(1)}, u32[]{:S(2)}, u32[]{:S(2)}) collective-permute-start(f32[2,64,128]{2,1,0:T(8,128)S(1)} %gram.1), channel_id=1, source_target_pairs={{0,1},{1,0},{2,3},{3,2},{4,5},{5,4},{6,7},{7,6},{8,9},{9,8},{10,11... | collective-permute-start | bytes 196616 | tf_op jit(solution)/shard_map/ppermute | solution.py:313
  67.1 7.1 %collective-permute-start.1 = (f32[2,64,128]{2,1,0:T(8,128)S(1)}, f32[2,64,128]{2,1,0:T(8,128)S(1)}, u32[]{:S(2)}, u32[]{:S(2)}) collective-permute-start(f32[2,64,128]{2,1,0:T(8,128)S(1)} %add.3.ga_ref), channel_id=1, source_target_pairs={{0,2},{2,0},{1,3},{3,1},{4,6},{6,4},{5,7},{7,5},{8,10},{10,8},{9,1... | collective-permute-start | bytes 196616 | tf_op jit(solution)/shard_map/ppermute | solution.py:314

commit v2 on v1

--- a/solution.py
+++ b/solution.py
@@ -15,6 +15,7 @@
 NF = 256
 DAMPING = 0.5
 QUARTER = NT // 4
+EIGHTH = NT // 8
 LANES = 128
 CH_TILE = 256
 FOLD_ROWS = 16
@@ -33,25 +34,31 @@
 
 
 def dft_tables():
-    t = np.arange(QUARTER, dtype=np.int64)
-    owners = np.arange(NWT, dtype=np.int64)
     scale = 1.0 / math.sqrt(NT)
 
-    def trig(f):
-        k = 4 * owners + 1 + f
+    def trig(f, owners, samples):
+        k = 4 * np.arange(NWT, dtype=np.int64)[owners] + 1 + f
+        t = np.arange(samples, dtype=np.int64)
         angle = (k[:, None] * t[None, :] % NT).astype(np.float64) * (2.0 * math.pi / NT)
         return np.cos(angle) * scale, np.sin(angle) * scale
 
-    odd = []
-    for f, sign in ((0, 1.0), (2, -1.0)):
-        cos, sin = trig(f)
-        odd.append(np.concatenate([cos, -sign * sin], axis=1))
-        odd.append(np.concatenate([-sin, -sign * cos], axis=1))
-    even = []
+    tables = []
+    for first in (0, 1):
+        rows = []
+        for f, sign, parity in ((0, 1.0, first), (2, -1.0, 1 - first)):
+            cos, sin = trig(f, slice(parity, None, 2), EIGHTH)
+            rows.append(np.concatenate([cos, -sign * sin], axis=1))
+            rows.append(np.concatenate([-sin, -sign * cos], axis=1))
+        tables.append(split_table(np.concatenate(rows, axis=0)))
     for f in (1, 3):
-        cos, sin = trig(f)
-        even.append(split_table(np.concatenate([cos, -sin], axis=0)))
-    return np.concatenate([split_table(np.concatenate(odd, axis=0)), np.concatenate(even, axis=0)], axis=1)
+        cos, sin = trig(f, slice(None), QUARTER)
+        tables.append(split_table(np.concatenate([cos, -sin], axis=0)))
+    return np.concatenate(tables, axis=0)
+
+
+CLASS_ROWS = [
+    [(f, ri, first if f == 0 else 1 - first, 2) for f in (0, 2) for ri in range(2)] for first in (0, 1)
+] + [[(f, ri, 0, 1) for ri in range(2)] for f in (1, 3)]
 
 
 def split(x):
@@ -92,27 +99,21 @@
             x0, x1, x2, x3 = (
                 x_ref[pl.ds(first + r, FOLD_ROWS), pl.ds(q * QUARTER, QUARTER)] for q in range(4)
             )
-            sum0, sum1 = x0 + x2, x1 + x3
-            for k, y in enumerate((x0 - x2, x1 - x3, sum0 - sum1, sum0 + sum1)):
-                high, low = split(y)
-                high_ref[pl.ds(r, FOLD_ROWS), pl.ds(k * QUARTER, QUARTER)] = high
-                low_ref[pl.ds(r, FOLD_ROWS), pl.ds(k * QUARTER, QUARTER)] = low
-
-    def spectra(count):
-        def part(rows, table_col, col, size):
-            table = table_ref[pl.ds(*rows), pl.ds(table_col, size)]
-            cut = (pl.ds(0, count), pl.ds(col, size))
-            return table_dot(table, high_ref[cut], low_ref[cut])
-
-        odd = part((0, 512), 0, 0, 2 * QUARTER)
-        even1 = part((0, 256), 2 * QUARTER, 2 * QUARTER, QUARTER)
-        even3 = part((256, 256), 2 * QUARTER, 3 * QUARTER, QUARTER)
-        return (
-            (odd[0:64], odd[64:128]),
-            (even1[0:64], even1[64:128]),
-            (odd[128:192], odd[192:256]),
-            (even3[0:64], even3[64:128]),
-        )
+            sum0, sum1, dif0, dif1 = x0 + x2, x1 + x3, x0 - x2, x1 - x3
+            near0, far0, near1, far1 = dif0[:, :EIGHTH], dif0[:, EIGHTH:], dif1[:, :EIGHTH], dif1[:, EIGHTH:]
+            turn0, turn1 = (far0 - far1) * math.sqrt(0.5), (far0 + far1) * math.sqrt(0.5)
+            folded = (near0 + turn0, near1 + turn1, near0 - turn0, near1 - turn1, sum0 - sum1, sum0 + sum1)
+            col = 0
+            for y in folded:
+                cut = (pl.ds(r, FOLD_ROWS), pl.ds(col, y.shape[1]))
+                high_ref[cut], low_ref[cut] = split(y)
+                col += y.shape[1]
+
+    def table(c):
+        return table_ref[pl.ds(c * 2 * LANES, 2 * LANES), :]
+
+    def owner_rows(row, owner, step):
+        return pl.ds(row + owner * ROWS, NWT // step, stride=step * ROWS)
 
     @pl.loop(0, tiles)
     def _(i):
@@ -132,21 +133,33 @@
         def _():
             table_copy.wait()
 
-        spec = spectra(CH_TILE)
-        for f in range(BINS):
-            for ri in range(2):
+        for c, runs in enumerate(CLASS_ROWS):
+            cut = (slice(None), pl.ds(c * QUARTER, QUARTER))
+            spec = table_dot(table(c), high_ref[cut], low_ref[cut])
+            start = 0
+            for f, ri, owner, step in runs:
                 for j in range(CH_TILE // LANES):
                     row = (f * 2 + ri) * 6 + i * (CH_TILE // LANES) + j
-                    o_ref[pl.ds(row, NWT, stride=ROWS), :] = spec[f][ri][:, j * LANES : (j + 1) * LANES]
+                    o_ref[owner_rows(row, owner, step), :] = spec[
+                        start : start + NWT // step, j * LANES : (j + 1) * LANES
+                    ]
+                start += NWT // step
 
     up_copy.wait()
     fold(channels, NVS)
-    for ref in (high_ref, low_ref):
-        ref[pl.ds(NVS, NVS)] = ref[pl.ds(0, NVS)]
-    spec_up = spectra(2 * NVS)
-    left = lax.broadcasted_iota(jnp.int32, (NWT, LANES), 1) < 64
-    for f in range(BINS):
-        o_ref[pl.ds(ROWS_D + f, NWT, stride=ROWS), :] = jnp.where(left, spec_up[f][0], spec_up[f][1])
+    for c, runs in enumerate(CLASS_ROWS):
+        cut = (pl.ds(0, NVS), pl.ds(c * QUARTER, QUARTER))
+        both = dot_nt(jnp.concatenate([high_ref[cut], low_ref[cut]], axis=0), table(c))
+        spec = both[:NVS, :LANES] + both[:NVS, LANES:] + both[NVS:, :LANES]
+        turned = jnp.concatenate([spec, spec], axis=0).T
+        start = 0
+        for (f, _, owner, step), _ in zip(runs[::2], runs[1::2]):
+            count = NWT // step
+            left = lax.broadcasted_iota(jnp.int32, (count, LANES), 1) < 64
+            o_ref[owner_rows(ROWS_D + f, owner, step), :] = jnp.where(
+                left, turned[start : start + count], turned[start + count : start + 2 * count]
+            )
+            start += 2 * count
 
 
 def dft(x, up):
@@ -240,7 +253,7 @@
     return jnp.sum(a * b, axis=1, keepdims=True)
 
 
-def solve_kernel(high_ref, low_ref, start_ref, ga_ref, gb_ref, o_ref):
+def solve_kernel(high_ref, low_ref, start_ref, ga_ref, gb_ref, o_hbm, o_ref, o_sem):
     lane = lax.broadcasted_iota(jnp.int32, (NWT, LANES), 1)
     row = lax.broadcasted_iota(jnp.int32, (NWT, LANES), 0)
     col = lane % 64
@@ -266,6 +279,7 @@
     res = starts
     res_g = times_gram(res)
     res_gg = times_gram(res_g)
+    copies = []
     for f in range(BINS):
         dir0, dir0_g, dir0_gg = res[f], res_g[f], res_gg[f]
         norm0 = row_dot(dir0, dir0_g)
@@ -287,12 +301,18 @@
         out = both[:LANES] + both[LANES:] + dot_nn(lhs_h, low_ref[f])
         o_ref[f, 0] = out[:64]
         o_ref[f, 1] = out[64:]
+        copies.append(pltpu.make_async_copy(o_ref.at[f], o_hbm.at[f], o_sem.at[f]))
+        copies[f].start()
+    for copy in copies:
+        copy.wait()
 
 
 def solve(prepared, gram_a, gram_b, channels):
     return pl.pallas_call(
         solve_kernel,
         out_shape=jax.ShapeDtypeStruct((BINS, 2, NVS, channels), F32),
+        out_specs=pl.BlockSpec(memory_space=pltpu.HBM),
+        scratch_shapes=[pltpu.VMEM((BINS, 2, NVS, channels), F32), pltpu.SemaphoreType.DMA((BINS,))],
         compiler_params=pltpu.CompilerParams(vmem_limit_bytes=40 << 20),
         cost_estimate=pl.CostEstimate(flops=3 * 10**8, bytes_accessed=4 * 10**6, transcendentals=0),
         name="solve",

time: 77.7 us -> 76.7 us (0.987)
  Pallas kernels: 12.7 us -> 11.6 us
where the time goes in v2:
time: 76.7 us; the launch traced here: 76 us
  blocking collectives  54.4 us (71%)
  Pallas kernels  11.6 us (15%)
  starting transfers between devices  6.71 us (9%)
  waiting for transfers between devices  3.25 us (4%)
    all_to_all x1, blocking collectives, body(): recv = lax.all_to_all(sent, 'win', split_axis=0, concat_axis=0, tiled=True)  54.4 us
    pallas_call x1, Pallas kernels, dft(): pl.pallas_call(dft_kernel, out_shape=pltpu.VMEM((NWT * ROWS, LANES), F32)...  7.81 us
    ppermute x1, starting transfers between devices, body(): far = lax.ppermute(chip, 'row', FAR_PAIRS)  4.3 us
    pallas_call x1, Pallas kernels, solve(): pl.pallas_call(solve_kernel, out_shape=jax.ShapeDtypeStruct((BINS, 2, NVS...  2.5 us
    ppermute x1, starting transfers between devices, body(): chip = part + lax.ppermute(part, 'row', CORE_PAIRS)  2.41 us
    ppermute x1, waiting for transfers between devices, body(): far = lax.ppermute(chip, 'row', FAR_PAIRS)  2.34 us
  transfers between devices with their start and end apart: 2, of which 2 were waited for; matrix products, arithmetic and copies ran while one was open for 0% of the time, Pallas kernels for 1%

profile of v2, /device:TPU:1, one launch (start us, length us, event | category | flops | bytes accessed | tf_op | source)
XLA Modules:
  0.0 76.0 jit_solution(13173147925479072550)
XLA Ops:
  0.0 7.8 %dft.1 = f32[3328,128]{1,0:T(8,128)S(1)} custom-call(f32[768,3072]{1,0:T(8,128)} %bitcast.7, f32[64,3072]{1,0:T(8,128)} %bitcast.8, bf16[1024,768]{1,0:T(8,128)(2,1)} %constant.2.clone.table_hbm), custom_call_target="tpu_custom_call" | custom-call | flops 3000000000 | bytes 15000000 | tf_op jit(solution)/shard_map/dft/pallas_call | solution.py:169
  7.8 54.4 %all_to_all.5 = f32[64,13,4,128]{3,2,1,0:T(4,128)S(1)} all-to-all(f32[64,13,4,128]{3,2,1,0:T(4,128)S(1)} %bitcast.6), channel_id=1, replica_groups=mesh['win'=64,'row'=4] {'win'}, dimensions={0} | all-to-all | bytes 3407872 | tf_op jit(solution)/shard_map/all_to_all | solution.py:330
  62.3 0.8 %gram.1 = f32[2,64,128]{2,1,0:T(8,128)S(1)} custom-call(f32[3328,128]{1,0:T(8,128)S(1)} %bitcast.4), custom_call_target="tpu_custom_call" | custom-call | flops 300000000 | bytes 2000000 | tf_op jit(solution)/shard_map/gram/pallas_call | solution.py:218
  63.1 2.4 %collective-permute-start = (f32[2,64,128]{2,1,0:T(8,128)S(1)}, f32[2,64,128]{2,1,0:T(8,128)S(1)}, u32[]{:S(2)}, u32[]{:S(2)}) collective-permute-start(f32[2,64,128]{2,1,0:T(8,128)S(1)} %gram.1), channel_id=1, source_target_pairs={{0,1},{1,0},{2,3},{3,2},{4,5},{5,4},{6,7},{7,6},{8,9},{9,8},{10,11... | collective-permute-start | bytes 196616 | tf_op jit(solution)/shard_map/ppermute | solution.py:333
  65.5 0.9 %collective-permute-done = f32[2,64,128]{2,1,0:T(8,128)S(1)} collective-permute-done((f32[2,64,128]{2,1,0:T(8,128)S(1)}, f32[2,64,128]{2,1,0:T(8,128)S(1)}, u32[]{:S(2)}, u32[]{:S(2)}) %collective-permute-start) | collective-permute-done | bytes 65568 | tf_op jit(solution)/shard_map/ppermute | solution.py:333
  66.4 4.3 %collective-permute-start.1 = (f32[2,64,128]{2,1,0:T(8,128)S(1)}, f32[2,64,128]{2,1,0:T(8,128)S(1)}, u32[]{:S(2)}, u32[]{:S(2)}) collective-permute-start(f32[2,64,128]{2,1,0:T(8,128)S(1)} %add.3.ga_ref), channel_id=1, source_target_pairs={{0,2},{2,0},{1,3},{3,1},{4,6},{6,4},{5,7},{7,5},{8,10},{10,8},{9,1... | collective-permute-start | bytes 196616 | tf_op jit(solution)/shard_map/ppermute | solution.py:334
  70.7 0.5 prep.1
  71.2 2.3 %collective-permute-done.1.gb_ref = f32[2,64,128]{2,1,0:T(8,128)S(1)} collective-permute-done((f32[2,64,128]{2,1,0:T(8,128)S(1)}, f32[2,64,128]{2,1,0:T(8,128)S(1)}, u32[]{:S(2)}, u32[]{:S(2)}) %collective-permute-start.1) | collective-permute-done | bytes 65568 | tf_op jit(solution)/shard_map/ppermute | solution.py:334
  73.5 2.5 %solve.1 = f32[4,2,64,768]{3,2,1,0:T(8,128)} custom-call(bf16[4,128,768]{2,1,0:T(8,128)(2,1)S(1)} %get-tuple-element.8.high_ref, bf16[4,128,768]{2,1,0:T(8,128)(2,1)S(1)} %get-tuple-element.9.low_ref, f32[4,64,128]{2,1,0:T(8,128)S(1)} %get-tuple-element.10.start_ref, f32[2,64,128]{2,1,0:T(8,128)S(1)} %add.3.ga_ref, ...), custom_call_target="tpu_custom_call" | custom-call | flops 300000000 | bytes 4000000 | tf_op jit(solution)/shard_map/solve/pallas_call | solution.py:311
  (1 shorter events, 0.0 us)
Async XLA Ops:
  63.1 3.3 %collective-permute-start = (f32[2,64,128]{2,1,0:T(8,128)S(1)}, f32[2,64,128]{2,1,0:T(8,128)S(1)}, u32[]{:S(2)}, u32[]{:S(2)}) collective-permute-start(f32[2,64,128]{2,1,0:T(8,128)S(1)} %gram.1), channel_id=1, source_target_pairs={{0,1},{1,0},{2,3},{3,2},{4,5},{5,4},{6,7},{7,6},{8,9},{9,8},{10,11... | collective-permute-start | bytes 196616 | tf_op jit(solution)/shard_map/ppermute | solution.py:333
  66.4 7.1 %collective-permute-start.1 = (f32[2,64,128]{2,1,0:T(8,128)S(1)}, f32[2,64,128]{2,1,0:T(8,128)S(1)}, u32[]{:S(2)}, u32[]{:S(2)}) collective-permute-start(f32[2,64,128]{2,1,0:T(8,128)S(1)} %add.3.ga_ref), channel_id=1, source_target_pairs={{0,2},{2,0},{1,3},{3,1},{4,6},{6,4},{5,7},{7,5},{8,10},{10,8},{9,1... | collective-permute-start | bytes 196616 | tf_op jit(solution)/shard_map/ppermute | solution.py:334

commit v3 on v2

--- a/solution.py
+++ b/solution.py
@@ -22,7 +22,8 @@
 VMEM_LIMIT = 60 << 20
 BINS = 4
 ROWS_D = 2 * BINS * 6
-ROWS = ROWS_D + BINS
+ROWS = ROWS_D + 2
+HALF_VS = NVS // 2
 F32 = jnp.float32
 BF16 = jnp.bfloat16
 
@@ -80,6 +81,16 @@
     return both[:half] + both[half:] + dot_nt(table[:half], low)
 
 
+def core_index():
+    return lax.rem(lax.axis_index("row"), 2)
+
+
+def lane_quarters(parts):
+    lane = lax.broadcasted_iota(jnp.int32, parts[0].shape, 1)
+    halves = [jnp.where(lane % 64 < HALF_VS, parts[k], parts[k + 1]) for k in (0, 2)]
+    return jnp.where(lane < 64, *halves)
+
+
 def dft_kernel(x_hbm, up_hbm, table_hbm, o_ref, x_ref, table_ref, high_ref, low_ref, x_sem, up_sem, table_sem):
     channels = x_hbm.shape[0]
     tiles = channels // CH_TILE
@@ -88,11 +99,13 @@
         rows = pl.ds(pl.multiple_of(i * CH_TILE, CH_TILE), CH_TILE)
         return pltpu.make_async_copy(x_hbm.at[rows], x_ref.at[rows], x_sem.at[i])
 
-    up_copy = pltpu.make_async_copy(up_hbm, x_ref.at[pl.ds(channels, NVS)], up_sem)
+    up_rows = pl.ds(pl.multiple_of(core_index() * HALF_VS, HALF_VS), HALF_VS)
+    up_copy = pltpu.make_async_copy(up_hbm.at[up_rows], x_ref.at[pl.ds(channels, HALF_VS)], up_sem)
     table_copy = pltpu.make_async_copy(table_hbm, table_ref, table_sem)
     x_copy(0).start()
     table_copy.start()
     x_copy(1).start()
+    up_copy.start()
 
     def fold(first, count):
         for r in range(0, count, FOLD_ROWS):
@@ -115,17 +128,32 @@
     def owner_rows(row, owner, step):
         return pl.ds(row + owner * ROWS, NWT // step, stride=step * ROWS)
 
+    def upgoing():
+        fold(channels, HALF_VS)
+        turned = []
+        for c in range(len(CLASS_ROWS)):
+            cut = (pl.ds(0, HALF_VS), pl.ds(c * QUARTER, QUARTER))
+            both = dot_nt(jnp.concatenate([high_ref[cut], low_ref[cut]], axis=0), table(c))
+            spec = both[:HALF_VS, :LANES] + both[:HALF_VS, LANES:] + both[HALF_VS:, :LANES]
+            turned.append(jnp.concatenate([spec] * 4, axis=0).T)
+        for owner in range(2):
+            one, two = turned[owner], turned[1 - owner]
+            o_ref[owner_rows(ROWS_D, owner, 2), :] = lane_quarters([one[:32], one[32:64], two[64:96], two[96:]])
+        one, two = turned[2], turned[3]
+        o_ref[owner_rows(ROWS_D + 1, 0, 1), :] = lane_quarters([one[:64], one[64:], two[:64], two[64:]])
+
     @pl.loop(0, tiles)
     def _(i):
+        @pl.when(i == tiles - 1)
+        def _():
+            up_copy.wait()
+            upgoing()
+
         x_copy(i).wait()
 
         @pl.when(i + 2 < tiles)
         def _():
             x_copy(i + 2).start()
-
-        @pl.when(i + 2 == tiles)
-        def _():
-            up_copy.start()
 
         fold(pl.multiple_of(i * CH_TILE, CH_TILE), CH_TILE)
 
@@ -145,22 +173,6 @@
                     ]
                 start += NWT // step
 
-    up_copy.wait()
-    fold(channels, NVS)
-    for c, runs in enumerate(CLASS_ROWS):
-        cut = (pl.ds(0, NVS), pl.ds(c * QUARTER, QUARTER))
-        both = dot_nt(jnp.concatenate([high_ref[cut], low_ref[cut]], axis=0), table(c))
-        spec = both[:NVS, :LANES] + both[:NVS, LANES:] + both[NVS:, :LANES]
-        turned = jnp.concatenate([spec, spec], axis=0).T
-        start = 0
-        for (f, _, owner, step), _ in zip(runs[::2], runs[1::2]):
-            count = NWT // step
-            left = lax.broadcasted_iota(jnp.int32, (count, LANES), 1) < 64
-            o_ref[owner_rows(ROWS_D + f, owner, step), :] = jnp.where(
-                left, turned[start : start + count], turned[start + count : start + 2 * count]
-            )
-            start += 2 * count
-
 
 def dft(x, up):
     table = dft_tables()
@@ -171,7 +183,7 @@
         out_shape=pltpu.VMEM((NWT * ROWS, LANES), F32),
         in_specs=[in_hbm, in_hbm, in_hbm],
         scratch_shapes=[
-            pltpu.VMEM((channels + NVS, NT), F32),
+            pltpu.VMEM((channels + HALF_VS, NT), F32),
             pltpu.VMEM(table.shape, BF16),
             pltpu.VMEM((CH_TILE, NT), BF16),
             pltpu.VMEM((CH_TILE, NT), BF16),
@@ -212,28 +224,34 @@
         packed.append(jnp.where(upper == left, both, swapped))
     for pair in range(BINS // 2):
         g_ref[pair] = jnp.where(left, packed[2 * pair], packed[2 * pair + 1])
+        g_ref[BINS // 2 + pair] = r_ref[pl.ds(ROWS_D + pair, NWT, stride=ROWS), :]
 
 
 def gram(recv):
     return pl.pallas_call(
         gram_kernel,
-        out_shape=jax.ShapeDtypeStruct((BINS // 2, NWT, LANES), F32),
+        out_shape=jax.ShapeDtypeStruct((BINS, NWT, LANES), F32),
         compiler_params=pltpu.CompilerParams(vmem_limit_bytes=40 << 20),
         cost_estimate=pl.CostEstimate(flops=3 * 10**8, bytes_accessed=2 * 10**6, transcendentals=0),
         name="gram",
     )(recv)
 
 
-def prep_kernel(r_ref, high_ref, low_ref, start_ref):
-    left = lax.broadcasted_iota(jnp.int32, (NWT, LANES), 1) < 64
+def prep_kernel(r_ref, own_ref, got_ref, high_ref, low_ref, start_ref):
     for f in range(BINS):
         high_ref[f], low_ref[f] = bin_matrix(r_ref, f)
-        up = r_ref[pl.ds(ROWS_D + f, NWT, stride=ROWS), :]
-        turned = jnp.concatenate([up, up], axis=0).T
-        start_ref[f] = jnp.where(left, turned[:64], turned[64:]) * (1.0 / math.sqrt(NCH))
-
-
-def prep(recv, channels):
+    left = lax.broadcasted_iota(jnp.int32, (HALF_VS, LANES), 1) < 64
+    first = core_index() == 0
+    for pair in range(BINS // 2):
+        own, got = own_ref[BINS // 2 + pair], got_ref[BINS // 2 + pair]
+        for half, up in enumerate((jnp.where(first, own, got), jnp.where(first, got, own))):
+            turned = jnp.concatenate([up, up], axis=0).T * (1.0 / math.sqrt(NCH))
+            for k in range(2):
+                re, im = turned[k * 64 : k * 64 + 32], turned[k * 64 + 32 : k * 64 + 64]
+                start_ref[2 * k + pair, pl.ds(half * HALF_VS, HALF_VS)] = jnp.where(left, re, im)
+
+
+def prep(recv, own, got, channels):
     matrices = pltpu.VMEM((BINS, 2 * NWT, channels), BF16)
     return pl.pallas_call(
         prep_kernel,
@@ -241,7 +259,7 @@
         compiler_params=pltpu.CompilerParams(vmem_limit_bytes=40 << 20),
         cost_estimate=pl.CostEstimate(flops=10**7, bytes_accessed=4 * 10**6, transcendentals=0),
         name="prep",
-    )(recv)
+    )(recv, own, got)
 
 
 def dot3(a, b_h, b_l):
@@ -323,16 +341,20 @@
 FAR_PAIRS = [(0, 2), (2, 0), (1, 3), (3, 1)]
 
 
+def finish(recv, part, channels):
+    got = lax.ppermute(part, "row", CORE_PAIRS)
+    chip = part[: BINS // 2] + got[: BINS // 2]
+    far = lax.ppermute(chip, "row", FAR_PAIRS)
+    return solve(prep(recv, part, got, channels), chip, far, channels)
+
+
 def body(downgoing, upgoing):
     channels = downgoing.shape[1]
     sent = dft(downgoing[0], upgoing[0])
-    sent = sent.reshape(NWT, ROWS // 4, 4, LANES)
+    sent = sent.reshape(NWT, ROWS // 2, 2, LANES)
     recv = lax.all_to_all(sent, "win", split_axis=0, concat_axis=0, tiled=True)
     recv = recv.reshape(NWT * ROWS, LANES)
-    part = gram(recv)
-    chip = part + lax.ppermute(part, "row", CORE_PAIRS)
-    far = lax.ppermute(chip, "row", FAR_PAIRS)
-    return solve(prep(recv, channels), chip, far, channels)
+    return finish(recv, gram(recv), channels)
 
 
 def solution(mesh):

time: 76.7 us -> 76 us (level)
  blocking collectives: 54.4 us -> 53.1 us
    all_to_all x1, blocking collectives: 54.4 us -> 53.1 us  [body(): recv = lax.all_to_all(sent, 'win', split_axis=0, concat_axis=0, tiled=True)]
where the time goes in v3:
time: 76 us; the launch traced here: 75.4 us
  blocking collectives  53.1 us (70%)
  Pallas kernels  12.3 us (16%)
  starting transfers between devices  6.68 us (9%)
  waiting for transfers between devices  3.32 us (4%)
    all_to_all x1, blocking collectives, body(): recv = lax.all_to_all(sent, 'win', split_axis=0, concat_axis=0, tiled=True)  53.1 us
    pallas_call x1, Pallas kernels, dft(): pl.pallas_call(dft_kernel, out_shape=pltpu.VMEM((NWT * ROWS, LANES), F32)...  8.48 us
    ppermute x1, starting transfers between devices, finish(): far = lax.ppermute(chip, 'row', FAR_PAIRS)  4.3 us
    pallas_call x1, Pallas kernels, solve(): pl.pallas_call(solve_kernel, out_shape=jax.ShapeDtypeStruct((BINS, 2, NVS...  2.51 us
    ppermute x1, starting transfers between devices, finish(): got = lax.ppermute(part, 'row', CORE_PAIRS)  2.39 us
    ppermute x1, waiting for transfers between devices, finish(): far = lax.ppermute(chip, 'row', FAR_PAIRS)  2.34 us
  transfers between devices with their start and end apart: 2, of which 2 were waited for; matrix products, arithmetic and copies ran while one was open for 0% of the time, Pallas kernels for 1%

profile of v3, /device:TPU:1, one launch (start us, length us, event | category | flops | bytes accessed | tf_op | source)
XLA Modules:
  0.0 75.4 jit_solution(4601641451624083672)
XLA Ops:
  0.0 8.5 %dft.1 = f32[3200,128]{1,0:T(8,128)S(1)} custom-call(f32[768,3072]{1,0:T(8,128)} %bitcast.7, f32[64,3072]{1,0:T(8,128)} %bitcast.8, bf16[1024,768]{1,0:T(8,128)(2,1)} %constant.2.clone.table_hbm), custom_call_target="tpu_custom_call" | custom-call | flops 3000000000 | bytes 15000000 | tf_op jit(solution)/shard_map/dft/pallas_call | solution.py:181
  8.5 53.1 %all_to_all.5 = f32[64,25,2,128]{3,2,1,0:T(2,128)S(1)} all-to-all(f32[64,25,2,128]{3,2,1,0:T(2,128)S(1)} %bitcast.6), channel_id=1, replica_groups=mesh['win'=64,'row'=4] {'win'}, dimensions={0} | all-to-all | bytes 3276800 | tf_op jit(solution)/shard_map/all_to_all | solution.py:355
  61.6 0.8 %gram.1.own_ref = f32[4,64,128]{2,1,0:T(8,128)S(1)} custom-call(f32[3200,128]{1,0:T(8,128)S(1)} %bitcast.4), custom_call_target="tpu_custom_call" | custom-call | flops 300000000 | bytes 2000000 | tf_op jit(solution)/shard_map/gram/pallas_call | solution.py:231
  62.4 2.4 %collective-permute-start = (f32[4,64,128]{2,1,0:T(8,128)S(1)}, f32[4,64,128]{2,1,0:T(8,128)S(1)}, u32[]{:S(2)}, u32[]{:S(2)}) collective-permute-start(f32[4,64,128]{2,1,0:T(8,128)S(1)} %gram.1.own_ref), channel_id=1, source_target_pairs={{0,1},{1,0},{2,3},{3,2},{4,5},{5,4},{6,7},{7,6},{8,9},{9,8},{10,11... | collective-permute-start | bytes 393224 | tf_op jit(solution)/shard_map/ppermute | solution.py:345
  64.8 1.0 %collective-permute-done.got_ref = f32[4,64,128]{2,1,0:T(8,128)S(1)} collective-permute-done((f32[4,64,128]{2,1,0:T(8,128)S(1)}, f32[4,64,128]{2,1,0:T(8,128)S(1)}, u32[]{:S(2)}, u32[]{:S(2)}) %collective-permute-start) | collective-permute-done | bytes 131104 | tf_op jit(solution)/shard_map/ppermute | solution.py:345
  65.8 4.3 %collective-permute-start.1 = (f32[2,64,128]{2,1,0:T(8,128)S(1)}, f32[2,64,128]{2,1,0:T(8,128)S(1)}, u32[]{:S(2)}, u32[]{:S(2)}) collective-permute-start(f32[2,64,128]{2,1,0:T(8,128)S(1)} %slice_add_fusion.ga_ref), channel_id=1, source_target_pairs={{0,2},{2,0},{1,3},{3,1},{4,6},{6,4},{5,7},{7,5},{8,10},{10,8},{9,1... | collective-permute-start | bytes 196616 | tf_op jit(solution)/shard_map/ppermute | solution.py:347
  70.1 0.5 prep.1
  70.5 2.3 %collective-permute-done.1.gb_ref = f32[2,64,128]{2,1,0:T(8,128)S(1)} collective-permute-done((f32[2,64,128]{2,1,0:T(8,128)S(1)}, f32[2,64,128]{2,1,0:T(8,128)S(1)}, u32[]{:S(2)}, u32[]{:S(2)}) %collective-permute-start.1) | collective-permute-done | bytes 65568 | tf_op jit(solution)/shard_map/ppermute | solution.py:347
  72.9 2.5 %solve.1 = f32[4,2,64,768]{3,2,1,0:T(8,128)} custom-call(bf16[4,128,768]{2,1,0:T(8,128)(2,1)S(1)} %get-tuple-element.8.high_ref, bf16[4,128,768]{2,1,0:T(8,128)(2,1)S(1)} %get-tuple-element.9.low_ref, f32[4,64,128]{2,1,0:T(8,128)S(1)} %get-tuple-element.10.start_ref, f32[2,64,128]{2,1,0:T(8,128)S(1)} %slice_add_fusion.ga_ref, ...), custom_call_target="tpu_custom_call" | custom-call | flops 300000000 | bytes 4000000 | tf_op jit(solution)/shard_map/solve/pallas_call | solution.py:329
  (1 shorter events, 0.0 us)
Async XLA Ops:
  62.4 3.4 %collective-permute-start = (f32[4,64,128]{2,1,0:T(8,128)S(1)}, f32[4,64,128]{2,1,0:T(8,128)S(1)}, u32[]{:S(2)}, u32[]{:S(2)}) collective-permute-start(f32[4,64,128]{2,1,0:T(8,128)S(1)} %gram.1.own_ref), channel_id=1, source_target_pairs={{0,1},{1,0},{2,3},{3,2},{4,5},{5,4},{6,7},{7,6},{8,9},{9,8},{10,11... | collective-permute-start | bytes 393224 | tf_op jit(solution)/shard_map/ppermute | solution.py:345
  65.8 7.1 %collective-permute-start.1 = (f32[2,64,128]{2,1,0:T(8,128)S(1)}, f32[2,64,128]{2,1,0:T(8,128)S(1)}, u32[]{:S(2)}, u32[]{:S(2)}) collective-permute-start(f32[2,64,128]{2,1,0:T(8,128)S(1)} %slice_add_fusion.ga_ref), channel_id=1, source_target_pairs={{0,2},{2,0},{1,3},{3,1},{4,6},{6,4},{5,7},{7,5},{8,10},{10,8},{9,1... | collective-permute-start | bytes 196616 | tf_op jit(solution)/shard_map/ppermute | solution.py:347

commit v4 on v3

--- a/solution.py
+++ b/solution.py
@@ -102,10 +102,9 @@
     up_rows = pl.ds(pl.multiple_of(core_index() * HALF_VS, HALF_VS), HALF_VS)
     up_copy = pltpu.make_async_copy(up_hbm.at[up_rows], x_ref.at[pl.ds(channels, HALF_VS)], up_sem)
     table_copy = pltpu.make_async_copy(table_hbm, table_ref, table_sem)
+    up_copy.start()
+    table_copy.start()
     x_copy(0).start()
-    table_copy.start()
-    x_copy(1).start()
-    up_copy.start()
 
     def fold(first, count):
         for r in range(0, count, FOLD_ROWS):
@@ -142,13 +141,13 @@
         one, two = turned[2], turned[3]
         o_ref[owner_rows(ROWS_D + 1, 0, 1), :] = lane_quarters([one[:64], one[64:], two[:64], two[64:]])
 
+    up_copy.wait()
+    table_copy.wait()
+    x_copy(1).start()
+    upgoing()
+
     @pl.loop(0, tiles)
     def _(i):
-        @pl.when(i == tiles - 1)
-        def _():
-            up_copy.wait()
-            upgoing()
-
         x_copy(i).wait()
 
         @pl.when(i + 2 < tiles)
@@ -156,10 +155,6 @@
             x_copy(i + 2).start()
 
         fold(pl.multiple_of(i * CH_TILE, CH_TILE), CH_TILE)
-
-        @pl.when(i == 0)
-        def _():
-            table_copy.wait()
 
         for c, runs in enumerate(CLASS_ROWS):
             cut = (slice(None), pl.ds(c * QUARTER, QUARTER))

time: 76 us -> 74 us (0.974)
  Pallas kernels: 12.3 us -> 10.2 us
    pallas_call x1, Pallas kernels: 8.48 us -> 6.44 us  [dft(): pl.pallas_call(dft_kernel, out_shape=pltpu.VMEM((NWT * ROWS, LANES), F32)...]
where the time goes in v4:
time: 74 us; the launch traced here: 73.4 us
  blocking collectives  53.1 us (72%)
  Pallas kernels  10.2 us (14%)
  starting transfers between devices  6.69 us (9%)
  waiting for transfers between devices  3.32 us (4%)
    all_to_all x1, blocking collectives, body(): recv = lax.all_to_all(sent, 'win', split_axis=0, concat_axis=0, tiled=True)  53.1 us
    pallas_call x1, Pallas kernels, dft(): pl.pallas_call(dft_kernel, out_shape=pltpu.VMEM((NWT * ROWS, LANES), F32)...  6.44 us
    ppermute x1, starting transfers between devices, finish(): far = lax.ppermute(chip, 'row', FAR_PAIRS)  4.3 us
    pallas_call x1, Pallas kernels, solve(): pl.pallas_call(solve_kernel, out_shape=jax.ShapeDtypeStruct((BINS, 2, NVS...  2.52 us
    ppermute x1, starting transfers between devices, finish(): got = lax.ppermute(part, 'row', CORE_PAIRS)  2.39 us
    ppermute x1, waiting for transfers between devices, finish(): far = lax.ppermute(chip, 'row', FAR_PAIRS)  2.34 us
  transfers between devices with their start and end apart: 2, of which 2 were waited for; matrix products, arithmetic and copies ran while one was open for 0% of the time, Pallas kernels for 1%

profile of v4, /device:TPU:1, one launch (start us, length us, event | category | flops | bytes accessed | tf_op | source)
XLA Modules:
  0.0 73.4 jit_solution(12978045476809585380)
XLA Ops:
  0.0 6.4 %dft.1 = f32[3200,128]{1,0:T(8,128)S(1)} custom-call(f32[768,3072]{1,0:T(8,128)} %bitcast.7, f32[64,3072]{1,0:T(8,128)} %bitcast.8, bf16[1024,768]{1,0:T(8,128)(2,1)} %constant.2.clone.table_hbm), custom_call_target="tpu_custom_call" | custom-call | flops 3000000000 | bytes 15000000 | tf_op jit(solution)/shard_map/dft/pallas_call | solution.py:176
  6.4 53.1 %all_to_all.5 = f32[64,25,2,128]{3,2,1,0:T(2,128)S(1)} all-to-all(f32[64,25,2,128]{3,2,1,0:T(2,128)S(1)} %bitcast.6), channel_id=1, replica_groups=mesh['win'=64,'row'=4] {'win'}, dimensions={0} | all-to-all | bytes 3276800 | tf_op jit(solution)/shard_map/all_to_all | solution.py:350
  59.5 0.8 %gram.1.own_ref = f32[4,64,128]{2,1,0:T(8,128)S(1)} custom-call(f32[3200,128]{1,0:T(8,128)S(1)} %bitcast.4), custom_call_target="tpu_custom_call" | custom-call | flops 300000000 | bytes 2000000 | tf_op jit(solution)/shard_map/gram/pallas_call | solution.py:226
  60.3 2.4 %collective-permute-start = (f32[4,64,128]{2,1,0:T(8,128)S(1)}, f32[4,64,128]{2,1,0:T(8,128)S(1)}, u32[]{:S(2)}, u32[]{:S(2)}) collective-permute-start(f32[4,64,128]{2,1,0:T(8,128)S(1)} %gram.1.own_ref), channel_id=1, source_target_pairs={{0,1},{1,0},{2,3},{3,2},{4,5},{5,4},{6,7},{7,6},{8,9},{9,8},{10,11... | collective-permute-start | bytes 393224 | tf_op jit(solution)/shard_map/ppermute | solution.py:340
  62.7 1.0 %collective-permute-done.got_ref = f32[4,64,128]{2,1,0:T(8,128)S(1)} collective-permute-done((f32[4,64,128]{2,1,0:T(8,128)S(1)}, f32[4,64,128]{2,1,0:T(8,128)S(1)}, u32[]{:S(2)}, u32[]{:S(2)}) %collective-permute-start) | collective-permute-done | bytes 131104 | tf_op jit(solution)/shard_map/ppermute | solution.py:340
  63.7 4.3 %collective-permute-start.1 = (f32[2,64,128]{2,1,0:T(8,128)S(1)}, f32[2,64,128]{2,1,0:T(8,128)S(1)}, u32[]{:S(2)}, u32[]{:S(2)}) collective-permute-start(f32[2,64,128]{2,1,0:T(8,128)S(1)} %slice_add_fusion.ga_ref), channel_id=1, source_target_pairs={{0,2},{2,0},{1,3},{3,1},{4,6},{6,4},{5,7},{7,5},{8,10},{10,8},{9,1... | collective-permute-start | bytes 196616 | tf_op jit(solution)/shard_map/ppermute | solution.py:342
  68.0 0.5 prep.1
  68.5 2.3 %collective-permute-done.1.gb_ref = f32[2,64,128]{2,1,0:T(8,128)S(1)} collective-permute-done((f32[2,64,128]{2,1,0:T(8,128)S(1)}, f32[2,64,128]{2,1,0:T(8,128)S(1)}, u32[]{:S(2)}, u32[]{:S(2)}) %collective-permute-start.1) | collective-permute-done | bytes 65568 | tf_op jit(solution)/shard_map/ppermute | solution.py:342
  70.8 2.5 %solve.1 = f32[4,2,64,768]{3,2,1,0:T(8,128)} custom-call(bf16[4,128,768]{2,1,0:T(8,128)(2,1)S(1)} %get-tuple-element.8.high_ref, bf16[4,128,768]{2,1,0:T(8,128)(2,1)S(1)} %get-tuple-element.9.low_ref, f32[4,64,128]{2,1,0:T(8,128)S(1)} %get-tuple-element.10.start_ref, f32[2,64,128]{2,1,0:T(8,128)S(1)} %slice_add_fusion.ga_ref, ...), custom_call_target="tpu_custom_call" | custom-call | flops 300000000 | bytes 4000000 | tf_op jit(solution)/shard_map/solve/pallas_call | solution.py:324
  (1 shorter events, 0.0 us)
Async XLA Ops:
  60.3 3.4 %collective-permute-start = (f32[4,64,128]{2,1,0:T(8,128)S(1)}, f32[4,64,128]{2,1,0:T(8,128)S(1)}, u32[]{:S(2)}, u32[]{:S(2)}) collective-permute-start(f32[4,64,128]{2,1,0:T(8,128)S(1)} %gram.1.own_ref), channel_id=1, source_target_pairs={{0,1},{1,0},{2,3},{3,2},{4,5},{5,4},{6,7},{7,6},{8,9},{9,8},{10,11... | collective-permute-start | bytes 393224 | tf_op jit(solution)/shard_map/ppermute | solution.py:340
  63.7 7.1 %collective-permute-start.1 = (f32[2,64,128]{2,1,0:T(8,128)S(1)}, f32[2,64,128]{2,1,0:T(8,128)S(1)}, u32[]{:S(2)}, u32[]{:S(2)}) collective-permute-start(f32[2,64,128]{2,1,0:T(8,128)S(1)} %slice_add_fusion.ga_ref), channel_id=1, source_target_pairs={{0,2},{2,0},{1,3},{3,1},{4,6},{6,4},{5,7},{7,5},{8,10},{10,8},{9,1... | collective-permute-start | bytes 196616 | tf_op jit(solution)/shard_map/ppermute | solution.py:342

commit v5 on v4

--- a/solution.py
+++ b/solution.py
@@ -232,7 +232,15 @@
     )(recv)
 
 
-def prep_kernel(r_ref, own_ref, got_ref, high_ref, low_ref, start_ref):
+def on_channels(y, high, low):
+    left = lax.broadcasted_iota(jnp.int32, y.shape, 1) < 64
+    turned = pltpu.roll(y, 64, 1)
+    y_high, y_low = split(jnp.concatenate([y, jnp.where(left, turned, -turned)], axis=0))
+    both = dot_nn(jnp.concatenate([y_high, y_low], axis=0), high)
+    return both[:LANES] + both[LANES:] + dot_nn(y_high, low)
+
+
+def prep_kernel(r_ref, own_ref, got_ref, high_ref, low_ref, start_ref, rhs_ref):
     for f in range(BINS):
         high_ref[f], low_ref[f] = bin_matrix(r_ref, f)
     left = lax.broadcasted_iota(jnp.int32, (HALF_VS, LANES), 1) < 64
@@ -244,13 +252,20 @@
             for k in range(2):
                 re, im = turned[k * 64 : k * 64 + 32], turned[k * 64 + 32 : k * 64 + 64]
                 start_ref[2 * k + pair, pl.ds(half * HALF_VS, HALF_VS)] = jnp.where(left, re, im)
+    for f in range(BINS):
+        rhs_ref[f] = on_channels(start_ref[f], high_ref[f], low_ref[f])
 
 
 def prep(recv, own, got, channels):
     matrices = pltpu.VMEM((BINS, 2 * NWT, channels), BF16)
     return pl.pallas_call(
         prep_kernel,
-        out_shape=(matrices, matrices, pltpu.VMEM((BINS, NVS, LANES), F32)),
+        out_shape=(
+            matrices,
+            matrices,
+            pltpu.VMEM((BINS, NVS, LANES), F32),
+            pltpu.VMEM((BINS, 2 * NVS, channels), F32),
+        ),
         compiler_params=pltpu.CompilerParams(vmem_limit_bytes=40 << 20),
         cost_estimate=pl.CostEstimate(flops=10**7, bytes_accessed=4 * 10**6, transcendentals=0),
         name="prep",
@@ -266,7 +281,7 @@
     return jnp.sum(a * b, axis=1, keepdims=True)
 
 
-def solve_kernel(high_ref, low_ref, start_ref, ga_ref, gb_ref, o_hbm, o_ref, o_sem):
+def solve_kernel(high_ref, low_ref, start_ref, rhs_ref, ga_ref, gb_ref, o_hbm, o_ref, o_sem):
     lane = lax.broadcasted_iota(jnp.int32, (NWT, LANES), 1)
     row = lax.broadcasted_iota(jnp.int32, (NWT, LANES), 0)
     col = lane % 64
@@ -292,6 +307,7 @@
     res = starts
     res_g = times_gram(res)
     res_gg = times_gram(res_g)
+    products = [on_channels(res_g[f], high_ref[f], low_ref[f]) for f in range(BINS)]
     copies = []
     for f in range(BINS):
         dir0, dir0_g, dir0_gg = res[f], res_g[f], res_gg[f]
@@ -307,11 +323,10 @@
         dir1_g = res1_g + ratio * dir0_g
         img1 = dir1_g * (1.0 / NCH) + DAMPING * dir1
         step1 = norm1 / row_dot(dir1_g, img1)
-        filt = (step0 * dir0 + step1 * dir1) * math.sqrt(NCH / NWT)
-        turned = pltpu.roll(filt, 64, 1)
-        lhs_h, lhs_l = split(jnp.concatenate([filt, jnp.where(left, turned, -turned)], axis=0))
-        both = dot_nn(jnp.concatenate([lhs_h, lhs_l], axis=0), high_ref[f])
-        out = both[:LANES] + both[LANES:] + dot_nn(lhs_h, low_ref[f])
+        scale = math.sqrt(NCH / NWT)
+        on_start = (step0 + step1 * (1.0 + ratio - DAMPING * step0)) * scale
+        on_image = (step1 * step0) * (-scale / NCH)
+        out = jnp.concatenate([on_start] * 2, axis=0) * rhs_ref[f] + jnp.concatenate([on_image] * 2, axis=0) * products[f]
         o_ref[f, 0] = out[:64]
         o_ref[f, 1] = out[64:]
         copies.append(pltpu.make_async_copy(o_ref.at[f], o_hbm.at[f], o_sem.at[f]))

time: 74 us -> 73.4 us (level)
  no operation moved by 1% of the time
where the time goes in v5:
time: 73.4 us; the launch traced here: 72.8 us
  blocking collectives  53.1 us (72%)
  Pallas kernels  10.1 us (14%)
  starting transfers between devices  6.69 us (9%)
  waiting for transfers between devices  2.88 us (4%)
    all_to_all x1, blocking collectives, body(): recv = lax.all_to_all(sent, 'win', split_axis=0, concat_axis=0, tiled=True)  53.1 us
    pallas_call x1, Pallas kernels, dft(): pl.pallas_call(dft_kernel, out_shape=pltpu.VMEM((NWT * ROWS, LANES), F32)...  6.44 us
    ppermute x1, starting transfers between devices, finish(): far = lax.ppermute(chip, 'row', FAR_PAIRS)  4.3 us
    ppermute x1, starting transfers between devices, finish(): got = lax.ppermute(part, 'row', CORE_PAIRS)  2.39 us
    pallas_call x1, Pallas kernels, solve(): pl.pallas_call(solve_kernel, out_shape=jax.ShapeDtypeStruct((BINS, 2, NVS...  1.93 us
    ppermute x1, waiting for transfers between devices, finish(): far = lax.ppermute(chip, 'row', FAR_PAIRS)  1.89 us
  transfers between devices with their start and end apart: 2, of which 2 were waited for; matrix products, arithmetic and copies ran while one was open for 0% of the time, Pallas kernels for 1%

profile of v5, /device:TPU:1, one launch (start us, length us, event | category | flops | bytes accessed | tf_op | source)
XLA Modules:
  0.0 72.8 jit_solution(4462584626512839785)
XLA Ops:
  0.0 6.4 %dft.1 = f32[3200,128]{1,0:T(8,128)S(1)} custom-call(f32[768,3072]{1,0:T(8,128)} %bitcast.7, f32[64,3072]{1,0:T(8,128)} %bitcast.8, bf16[1024,768]{1,0:T(8,128)(2,1)} %constant.2.clone.table_hbm), custom_call_target="tpu_custom_call" | custom-call | flops 3000000000 | bytes 15000000 | tf_op jit(solution)/shard_map/dft/pallas_call | solution.py:176
  6.4 53.1 %all_to_all.5 = f32[64,25,2,128]{3,2,1,0:T(2,128)S(1)} all-to-all(f32[64,25,2,128]{3,2,1,0:T(2,128)S(1)} %bitcast.6), channel_id=1, replica_groups=mesh['win'=64,'row'=4] {'win'}, dimensions={0} | all-to-all | bytes 3276800 | tf_op jit(solution)/shard_map/all_to_all | solution.py:365
  59.5 0.8 %gram.1.own_ref = f32[4,64,128]{2,1,0:T(8,128)S(1)} custom-call(f32[3200,128]{1,0:T(8,128)S(1)} %bitcast.4), custom_call_target="tpu_custom_call" | custom-call | flops 300000000 | bytes 2000000 | tf_op jit(solution)/shard_map/gram/pallas_call | solution.py:226
  60.3 2.4 %collective-permute-start = (f32[4,64,128]{2,1,0:T(8,128)S(1)}, f32[4,64,128]{2,1,0:T(8,128)S(1)}, u32[]{:S(2)}, u32[]{:S(2)}) collective-permute-start(f32[4,64,128]{2,1,0:T(8,128)S(1)} %gram.1.own_ref), channel_id=1, source_target_pairs={{0,1},{1,0},{2,3},{3,2},{4,5},{5,4},{6,7},{7,6},{8,9},{9,8},{10,11... | collective-permute-start | bytes 393224 | tf_op jit(solution)/shard_map/ppermute | solution.py:355
  62.7 1.0 %collective-permute-done.got_ref = f32[4,64,128]{2,1,0:T(8,128)S(1)} collective-permute-done((f32[4,64,128]{2,1,0:T(8,128)S(1)}, f32[4,64,128]{2,1,0:T(8,128)S(1)}, u32[]{:S(2)}, u32[]{:S(2)}) %collective-permute-start) | collective-permute-done | bytes 131104 | tf_op jit(solution)/shard_map/ppermute | solution.py:355
  63.7 4.3 %collective-permute-start.1 = (f32[2,64,128]{2,1,0:T(8,128)S(1)}, f32[2,64,128]{2,1,0:T(8,128)S(1)}, u32[]{:S(2)}, u32[]{:S(2)}) collective-permute-start(f32[2,64,128]{2,1,0:T(8,128)S(1)} %slice_add_fusion.ga_ref), channel_id=1, source_target_pairs={{0,2},{2,0},{1,3},{3,1},{4,6},{6,4},{5,7},{7,5},{8,10},{10,8},{9,1... | collective-permute-start | bytes 196616 | tf_op jit(solution)/shard_map/ppermute | solution.py:357
  68.0 0.9 %prep.1 = (bf16[4,128,768]{2,1,0:T(8,128)(2,1)S(1)}, bf16[4,128,768]{2,1,0:T(8,128)(2,1)S(1)}, f32[4,64,128]{2,1,0:T(8,128)S(1)}, f32[4,128,768]{2,1,0:T(8,128)S(1)}) custom-call(f32[3200,128]{1,0:T(8,128)S(1)} %bitcast.5, f32[4,64,128]{2,1,0:T(8,128)S(1)} %gram.1.own_ref, f32[4,64,128]{2,1,0:T(8,128)S(1)} %collective-permute-done.got_ref), custom_call_target="tpu_custom_call" | custom-call | flops 10000000 | bytes 4000000 | tf_op jit(solution)/shard_map/prep/pallas_call | solution.py:261
  68.9 1.9 %collective-permute-done.1.gb_ref = f32[2,64,128]{2,1,0:T(8,128)S(1)} collective-permute-done((f32[2,64,128]{2,1,0:T(8,128)S(1)}, f32[2,64,128]{2,1,0:T(8,128)S(1)}, u32[]{:S(2)}, u32[]{:S(2)}) %collective-permute-start.1) | collective-permute-done | bytes 65568 | tf_op jit(solution)/shard_map/ppermute | solution.py:357
  70.8 1.9 %solve.1 = f32[4,2,64,768]{3,2,1,0:T(8,128)} custom-call(bf16[4,128,768]{2,1,0:T(8,128)(2,1)S(1)} %get-tuple-element.9.high_ref, bf16[4,128,768]{2,1,0:T(8,128)(2,1)S(1)} %get-tuple-element.10.low_ref, f32[4,64,128]{2,1,0:T(8,128)S(1)} %get-tuple-element.11.start_ref, f32[4,128,768]{2,1,0:T(8,128)S(1)} %get-tuple-element.12.rhs_ref, ...), custom_call_target="tpu_custom_call" | custom-call | flops 300000000 | bytes 4000000 | tf_op jit(solution)/shard_map/solve/pallas_call | solution.py:339
  (1 shorter events, 0.0 us)
Async XLA Ops:
  60.3 3.4 %collective-permute-start = (f32[4,64,128]{2,1,0:T(8,128)S(1)}, f32[4,64,128]{2,1,0:T(8,128)S(1)}, u32[]{:S(2)}, u32[]{:S(2)}) collective-permute-start(f32[4,64,128]{2,1,0:T(8,128)S(1)} %gram.1.own_ref), channel_id=1, source_target_pairs={{0,1},{1,0},{2,3},{3,2},{4,5},{5,4},{6,7},{7,6},{8,9},{9,8},{10,11... | collective-permute-start | bytes 393224 | tf_op jit(solution)/shard_map/ppermute | solution.py:355
  63.7 7.1 %collective-permute-start.1 = (f32[2,64,128]{2,1,0:T(8,128)S(1)}, f32[2,64,128]{2,1,0:T(8,128)S(1)}, u32[]{:S(2)}, u32[]{:S(2)}) collective-permute-start(f32[2,64,128]{2,1,0:T(8,128)S(1)} %slice_add_fusion.ga_ref), channel_id=1, source_target_pairs={{0,2},{2,0},{1,3},{3,1},{4,6},{6,4},{5,7},{7,5},{8,10},{10,8},{9,1... | collective-permute-start | bytes 196616 | tf_op jit(solution)/shard_map/ppermute | solution.py:357

commit v6 on v5

--- a/solution.py
+++ b/solution.py
@@ -1,3 +1,4 @@
+import functools
 import math
 
 import jax
@@ -202,13 +203,13 @@
     return split(jnp.concatenate([bin_rows(r_ref, f, 0), bin_rows(r_ref, f, 1)], axis=0))
 
 
-def gram_kernel(r_ref, g_ref):
+def gram_kernel(pair, r_ref, g_ref):
     lane = lax.broadcasted_iota(jnp.int32, (NWT, LANES), 1)
     row = lax.broadcasted_iota(jnp.int32, (NWT, LANES), 0)
     upper = row <= lane % 64
     left = lane < 64
     packed = []
-    for f in range(BINS):
+    for f in (2 * pair, 2 * pair + 1):
         high, low = bin_matrix(r_ref, f)
         both = dot_nt(jnp.concatenate([high, low], axis=0), high)
         cross = both[LANES:]
@@ -217,18 +218,21 @@
         both = total[:64] + jnp.where(left, below, -below)
         swapped = pltpu.roll(both, 64, 1)
         packed.append(jnp.where(upper == left, both, swapped))
-    for pair in range(BINS // 2):
-        g_ref[pair] = jnp.where(left, packed[2 * pair], packed[2 * pair + 1])
-        g_ref[BINS // 2 + pair] = r_ref[pl.ds(ROWS_D + pair, NWT, stride=ROWS), :]
+    g_ref[0] = jnp.where(left, packed[0], packed[1])
+    g_ref[1] = r_ref[pl.ds(ROWS_D + pair, NWT, stride=ROWS), :]
 
 
 def gram(recv):
+    return [gram_pair(recv, pair) for pair in range(BINS // 2)]
+
+
+def gram_pair(recv, pair):
     return pl.pallas_call(
-        gram_kernel,
-        out_shape=jax.ShapeDtypeStruct((BINS, NWT, LANES), F32),
+        functools.partial(gram_kernel, pair),
+        out_shape=jax.ShapeDtypeStruct((2, NWT, LANES), F32),
         compiler_params=pltpu.CompilerParams(vmem_limit_bytes=40 << 20),
         cost_estimate=pl.CostEstimate(flops=3 * 10**8, bytes_accessed=2 * 10**6, transcendentals=0),
-        name="gram",
+        name=f"gram{pair}",
     )(recv)
 
 
@@ -240,13 +244,13 @@
     return both[:LANES] + both[LANES:] + dot_nn(y_high, low)
 
 
-def prep_kernel(r_ref, own_ref, got_ref, high_ref, low_ref, start_ref, rhs_ref):
+def prep_kernel(r_ref, own0_ref, got0_ref, own1_ref, got1_ref, high_ref, low_ref, start_ref, rhs_ref):
     for f in range(BINS):
         high_ref[f], low_ref[f] = bin_matrix(r_ref, f)
     left = lax.broadcasted_iota(jnp.int32, (HALF_VS, LANES), 1) < 64
     first = core_index() == 0
-    for pair in range(BINS // 2):
-        own, got = own_ref[BINS // 2 + pair], got_ref[BINS // 2 + pair]
+    for pair, refs in enumerate(((own0_ref, got0_ref), (own1_ref, got1_ref))):
+        own, got = (ref[1] for ref in refs)
         for half, up in enumerate((jnp.where(first, own, got), jnp.where(first, got, own))):
             turned = jnp.concatenate([up, up], axis=0).T * (1.0 / math.sqrt(NCH))
             for k in range(2):
@@ -256,7 +260,7 @@
         rhs_ref[f] = on_channels(start_ref[f], high_ref[f], low_ref[f])
 
 
-def prep(recv, own, got, channels):
+def prep(recv, parts, gots, channels):
     matrices = pltpu.VMEM((BINS, 2 * NWT, channels), BF16)
     return pl.pallas_call(
         prep_kernel,
@@ -269,7 +273,7 @@
         compiler_params=pltpu.CompilerParams(vmem_limit_bytes=40 << 20),
         cost_estimate=pl.CostEstimate(flops=10**7, bytes_accessed=4 * 10**6, transcendentals=0),
         name="prep",
-    )(recv, own, got)
+    )(recv, parts[0], gots[0], parts[1], gots[1])
 
 
 def dot3(a, b_h, b_l):
@@ -281,14 +285,14 @@
     return jnp.sum(a * b, axis=1, keepdims=True)
 
 
-def solve_kernel(high_ref, low_ref, start_ref, rhs_ref, ga_ref, gb_ref, o_hbm, o_ref, o_sem):
+def solve_kernel(high_ref, low_ref, start_ref, rhs_ref, ga0_ref, ga1_ref, gb0_ref, gb1_ref, o_hbm, o_ref, o_sem):
     lane = lax.broadcasted_iota(jnp.int32, (NWT, LANES), 1)
     row = lax.broadcasted_iota(jnp.int32, (NWT, LANES), 0)
     col = lane % 64
     left = lane < 64
     grams = []
-    for pair in range(BINS // 2):
-        packed = ga_ref[pair] + gb_ref[pair]
+    for ga_ref, gb_ref in ((ga0_ref, gb0_ref), (ga1_ref, gb1_ref)):
+        packed = ga_ref[...] + gb_ref[...]
         turned = jnp.concatenate([packed, packed], axis=0).T
         other = pltpu.roll(packed, 64, 1)
         for half in range(2):
@@ -335,7 +339,7 @@
         copy.wait()
 
 
-def solve(prepared, gram_a, gram_b, channels):
+def solve(prepared, chips, fars, channels):
     return pl.pallas_call(
         solve_kernel,
         out_shape=jax.ShapeDtypeStruct((BINS, 2, NVS, channels), F32),
@@ -344,18 +348,18 @@
         compiler_params=pltpu.CompilerParams(vmem_limit_bytes=40 << 20),
         cost_estimate=pl.CostEstimate(flops=3 * 10**8, bytes_accessed=4 * 10**6, transcendentals=0),
         name="solve",
-    )(*prepared, gram_a, gram_b)
+    )(*prepared, *chips, *fars)
 
 
 CORE_PAIRS = [(0, 1), (1, 0), (2, 3), (3, 2)]
 FAR_PAIRS = [(0, 2), (2, 0), (1, 3), (3, 1)]
 
 
-def finish(recv, part, channels):
-    got = lax.ppermute(part, "row", CORE_PAIRS)
-    chip = part[: BINS // 2] + got[: BINS // 2]
-    far = lax.ppermute(chip, "row", FAR_PAIRS)
-    return solve(prep(recv, part, got, channels), chip, far, channels)
+def finish(recv, parts, channels):
+    gots = [lax.ppermute(part, "row", CORE_PAIRS) for part in parts]
+    chips = [part[0] + got[0] for part, got in zip(parts, gots)]
+    fars = [lax.ppermute(chip, "row", FAR_PAIRS) for chip in chips]
+    return solve(prep(recv, parts, gots, channels), chips, fars, channels)
 
 
 def body(downgoing, upgoing):

time: 73.4 us -> 76.4 us (1.041)
  waiting for transfers between devices: 2.88 us -> 4.8 us
  starting transfers between devices: 6.69 us -> 7.95 us
    ppermute x2 -> x4, waiting for transfers between devices: 2.88 us -> 4.8 us  [the longest x2 4.59 us: finish(): fars = [lax.ppermute(chip, 'row', FAR_PAIRS) for chip in chips]]
    ppermute x2 -> x4, starting transfers between devices: 6.69 us -> 7.95 us  [the longest x2 5.46 us: finish(): fars = [lax.ppermute(chip, 'row', FAR_PAIRS) for chip in chips]]
  transfers between devices with their start and end apart: 2 -> 4, of which waited for: 2 -> 3; matrix products, arithmetic and copies ran while one was open for 0% -> 0% of each run, Pallas kernels for 1% -> 2%
where the time goes in v6:
time: 76.4 us; the launch traced here: 76.3 us
  blocking collectives  53.1 us (70%)
  Pallas kernels  10.4 us (14%)
  starting transfers between devices  7.95 us (10%)
  waiting for transfers between devices  4.8 us (6%)
    all_to_all x1, blocking collectives, body(): recv = lax.all_to_all(sent, 'win', split_axis=0, concat_axis=0, tiled=True)  53.1 us
    pallas_call x1, Pallas kernels, dft(): pl.pallas_call(dft_kernel, out_shape=pltpu.VMEM((NWT * ROWS, LANES), F32)...  6.44 us
    ppermute x2, starting transfers between devices, finish(): fars = [lax.ppermute(chip, 'row', FAR_PAIRS) for chip in chips]  5.46 us
    ppermute x2, waiting for transfers between devices, finish(): fars = [lax.ppermute(chip, 'row', FAR_PAIRS) for chip in chips]  4.59 us
    ppermute x2, starting transfers between devices, finish(): gots = [lax.ppermute(part, 'row', CORE_PAIRS) for part in parts]  2.49 us
    pallas_call x1, Pallas kernels, solve(): pl.pallas_call(solve_kernel, out_shape=jax.ShapeDtypeStruct((BINS, 2, NVS...  1.93 us
  transfers between devices with their start and end apart: 4, of which 3 were waited for; matrix products, arithmetic and copies ran while one was open for 0% of the time, Pallas kernels for 2%

profile of v6, /device:TPU:1, one launch (start us, length us, event | category | flops | bytes accessed | tf_op | source)
XLA Modules:
  0.0 76.3 jit_solution(17585715827575379462)
XLA Ops:
  0.0 6.4 %dft.1 = f32[3200,128]{1,0:T(8,128)S(1)} custom-call(f32[768,3072]{1,0:T(8,128)} %bitcast.12, f32[64,3072]{1,0:T(8,128)} %bitcast.13, bf16[1024,768]{1,0:T(8,128)(2,1)} %constant.2.clone.table_hbm), custom_call_target="tpu_custom_call" | custom-call | flops 3000000000 | bytes 15000000 | tf_op jit(solution)/shard_map/dft/pallas_call | solution.py:177
  6.4 53.1 %all_to_all.5 = f32[64,25,2,128]{3,2,1,0:T(2,128)S(1)} all-to-all(f32[64,25,2,128]{3,2,1,0:T(2,128)S(1)} %bitcast.11), channel_id=1, replica_groups=mesh['win'=64,'row'=4] {'win'}, dimensions={0} | all-to-all | bytes 3276800 | tf_op jit(solution)/shard_map/all_to_all | solution.py:369
  59.5 0.6 gram0.1.own0_ref
  60.1 2.4 %collective-permute-start = (f32[2,64,128]{2,1,0:T(8,128)S(1)}, f32[2,64,128]{2,1,0:T(8,128)S(1)}, u32[]{:S(2)}, u32[]{:S(2)}) collective-permute-start(f32[2,64,128]{2,1,0:T(8,128)S(1)} %gram0.1.own0_ref), channel_id=1, source_target_pairs={{0,1},{1,0},{2,3},{3,2},{4,5},{5,4},{6,7},{7,6},{8,9},{9,8},{10,11... | collective-permute-start | bytes 196616 | tf_op jit(solution)/shard_map/ppermute | solution.py:359
  62.5 0.6 gram1.1.own1_ref
  63.1 0.1 collective-permute-start.1
  63.2 0.2 collective-permute-done.got0_ref
  63.4 4.2 %collective-permute-start.2 = (f32[64,128]{1,0:T(8,128)S(1)}, f32[64,128]{1,0:T(8,128)S(1)}, u32[]{:S(2)}, u32[]{:S(2)}) collective-permute-start(f32[64,128]{1,0:T(8,128)S(1)} %fusion.1.ga0_ref), channel_id=1, source_target_pairs={{0,2},{2,0},{1,3},{3,1},{4,6},{6,4},{5,7},{7,5},{8,10},{10,8},{9,1... | collective-permute-start | bytes 98312 | tf_op jit(solution)/shard_map/ppermute | solution.py:361
  67.6 0.0 collective-permute-done.1.got1_ref
  67.6 1.2 %collective-permute-start.3 = (f32[64,128]{1,0:T(8,128)S(1)}, f32[64,128]{1,0:T(8,128)S(1)}, u32[]{:S(2)}, u32[]{:S(2)}) collective-permute-start(f32[64,128]{1,0:T(8,128)S(1)} %fusion.ga1_ref), channel_id=1, source_target_pairs={{0,2},{2,0},{1,3},{3,1},{4,6},{6,4},{5,7},{7,5},{8,10},{10,8},{9,1... | collective-permute-start | bytes 98312 | tf_op jit(solution)/shard_map/ppermute | solution.py:361
  68.9 0.9 %prep.1 = (bf16[4,128,768]{2,1,0:T(8,128)(2,1)S(1)}, bf16[4,128,768]{2,1,0:T(8,128)(2,1)S(1)}, f32[4,64,128]{2,1,0:T(8,128)S(1)}, f32[4,128,768]{2,1,0:T(8,128)S(1)}) custom-call(f32[3200,128]{1,0:T(8,128)S(1)} %bitcast.10, f32[2,64,128]{2,1,0:T(8,128)S(1)} %gram0.1.own0_ref, f32[2,64,128]{2,1,0:T(8,128)S(1)} %collective-permute-done.got0_ref, ...), custom_call_target="tpu_custom_call" | custom-call | flops 10000000 | bytes 4000000 | tf_op jit(solution)/shard_map/prep/pallas_call | solution.py:265
  69.8 0.3 collective-permute-done.2.gb0_ref
  70.1 4.3 %collective-permute-done.3.gb1_ref = f32[64,128]{1,0:T(8,128)S(1)} collective-permute-done((f32[64,128]{1,0:T(8,128)S(1)}, f32[64,128]{1,0:T(8,128)S(1)}, u32[]{:S(2)}, u32[]{:S(2)}) %collective-permute-start.3) | collective-permute-done | bytes 32800 | tf_op jit(solution)/shard_map/ppermute | solution.py:361
  74.4 1.9 %solve.1 = f32[4,2,64,768]{3,2,1,0:T(8,128)} custom-call(bf16[4,128,768]{2,1,0:T(8,128)(2,1)S(1)} %get-tuple-element.9.high_ref, bf16[4,128,768]{2,1,0:T(8,128)(2,1)S(1)} %get-tuple-element.10.low_ref, f32[4,64,128]{2,1,0:T(8,128)S(1)} %get-tuple-element.11.start_ref, f32[4,128,768]{2,1,0:T(8,128)S(1)} %get-tuple-element.12.rhs_ref, ...), custom_call_target="tpu_custom_call" | custom-call | flops 300000000 | bytes 4000000 | tf_op jit(solution)/shard_map/solve/pallas_call | solution.py:343
  (2 shorter events, 0.0 us)
Async XLA Ops:
  60.1 3.3 %collective-permute-start = (f32[2,64,128]{2,1,0:T(8,128)S(1)}, f32[2,64,128]{2,1,0:T(8,128)S(1)}, u32[]{:S(2)}, u32[]{:S(2)}) collective-permute-start(f32[2,64,128]{2,1,0:T(8,128)S(1)} %gram0.1.own0_ref), channel_id=1, source_target_pairs={{0,1},{1,0},{2,3},{3,2},{4,5},{5,4},{6,7},{7,6},{8,9},{9,8},{10,11... | collective-permute-start | bytes 196616 | tf_op jit(solution)/shard_map/ppermute | solution.py:359
  63.1 4.5 %collective-permute-start.1 = (f32[2,64,128]{2,1,0:T(8,128)S(1)}, f32[2,64,128]{2,1,0:T(8,128)S(1)}, u32[]{:S(2)}, u32[]{:S(2)}) collective-permute-start(f32[2,64,128]{2,1,0:T(8,128)S(1)} %gram1.1.own1_ref), channel_id=1, source_target_pairs={{0,1},{1,0},{2,3},{3,2},{4,5},{5,4},{6,7},{7,6},{8,9},{9,8},{10,11... | collective-permute-start | bytes 196616 | tf_op jit(solution)/shard_map/ppermute | solution.py:359
  63.4 6.7 %collective-permute-start.2 = (f32[64,128]{1,0:T(8,128)S(1)}, f32[64,128]{1,0:T(8,128)S(1)}, u32[]{:S(2)}, u32[]{:S(2)}) collective-permute-start(f32[64,128]{1,0:T(8,128)S(1)} %fusion.1.ga0_ref), channel_id=1, source_target_pairs={{0,2},{2,0},{1,3},{3,1},{4,6},{6,4},{5,7},{7,5},{8,10},{10,8},{9,1... | collective-permute-start | bytes 98312 | tf_op jit(solution)/shard_map/ppermute | solution.py:361
  67.6 6.8 %collective-permute-start.3 = (f32[64,128]{1,0:T(8,128)S(1)}, f32[64,128]{1,0:T(8,128)S(1)}, u32[]{:S(2)}, u32[]{:S(2)}) collective-permute-start(f32[64,128]{1,0:T(8,128)S(1)} %fusion.ga1_ref), channel_id=1, source_target_pairs={{0,2},{2,0},{1,3},{3,1},{4,6},{6,4},{5,7},{7,5},{8,10},{10,8},{9,1... | collective-permute-start | bytes 98312 | tf_op jit(solution)/shard_map/ppermute | solution.py:361

commit v7 on v5

--- a/solution.py
+++ b/solution.py
@@ -274,7 +274,8 @@
 
 def dot3(a, b_h, b_l):
     a_h, a_l = split(a)
-    return dot_nn(a_h, b_h) + dot_nn(a_l, b_h) + dot_nn(a_h, b_l)
+    both = dot_nn(jnp.concatenate([a_h, a_l], axis=0), b_h)
+    return both[: a.shape[0]] + both[a.shape[0] :] + dot_nn(a_h, b_l)
 
 
 def row_dot(a, b):

time: 73.4 us -> 73.4 us (level)
  no operation moved by 1% of the time
where the time goes in v7:
time: 73.4 us; the launch traced here: 72.7 us
  blocking collectives  53.1 us (72%)
  Pallas kernels  10.1 us (14%)
  starting transfers between devices  6.69 us (9%)
  waiting for transfers between devices  2.88 us (4%)
    all_to_all x1, blocking collectives, body(): recv = lax.all_to_all(sent, 'win', split_axis=0, concat_axis=0, tiled=True)  53.1 us
    pallas_call x1, Pallas kernels, dft(): pl.pallas_call(dft_kernel, out_shape=pltpu.VMEM((NWT * ROWS, LANES), F32)...  6.44 us
    ppermute x1, starting transfers between devices, finish(): far = lax.ppermute(chip, 'row', FAR_PAIRS)  4.3 us
    ppermute x1, starting transfers between devices, finish(): got = lax.ppermute(part, 'row', CORE_PAIRS)  2.39 us
    ppermute x1, waiting for transfers between devices, finish(): far = lax.ppermute(chip, 'row', FAR_PAIRS)  1.89 us
    pallas_call x1, Pallas kernels, solve(): pl.pallas_call(solve_kernel, out_shape=jax.ShapeDtypeStruct((BINS, 2, NVS...  1.89 us
  transfers between devices with their start and end apart: 2, of which 2 were waited for; matrix products, arithmetic and copies ran while one was open for 0% of the time, Pallas kernels for 1%

profile of v7, /device:TPU:1, one launch (start us, length us, event | category | flops | bytes accessed | tf_op | source)
XLA Modules:
  0.0 72.7 jit_solution(10687522639659572192)
XLA Ops:
  0.0 6.4 %dft.1 = f32[3200,128]{1,0:T(8,128)S(1)} custom-call(f32[768,3072]{1,0:T(8,128)} %bitcast.7, f32[64,3072]{1,0:T(8,128)} %bitcast.8, bf16[1024,768]{1,0:T(8,128)(2,1)} %constant.2.clone.table_hbm), custom_call_target="tpu_custom_call" | custom-call | flops 3000000000 | bytes 15000000 | tf_op jit(solution)/shard_map/dft/pallas_call | solution.py:176
  6.4 53.1 %all_to_all.5 = f32[64,25,2,128]{3,2,1,0:T(2,128)S(1)} all-to-all(f32[64,25,2,128]{3,2,1,0:T(2,128)S(1)} %bitcast.6), channel_id=1, replica_groups=mesh['win'=64,'row'=4] {'win'}, dimensions={0} | all-to-all | bytes 3276800 | tf_op jit(solution)/shard_map/all_to_all | solution.py:366
  59.5 0.8 %gram.1.own_ref = f32[4,64,128]{2,1,0:T(8,128)S(1)} custom-call(f32[3200,128]{1,0:T(8,128)S(1)} %bitcast.4), custom_call_target="tpu_custom_call" | custom-call | flops 300000000 | bytes 2000000 | tf_op jit(solution)/shard_map/gram/pallas_call | solution.py:226
  60.3 2.4 %collective-permute-start = (f32[4,64,128]{2,1,0:T(8,128)S(1)}, f32[4,64,128]{2,1,0:T(8,128)S(1)}, u32[]{:S(2)}, u32[]{:S(2)}) collective-permute-start(f32[4,64,128]{2,1,0:T(8,128)S(1)} %gram.1.own_ref), channel_id=1, source_target_pairs={{0,1},{1,0},{2,3},{3,2},{4,5},{5,4},{6,7},{7,6},{8,9},{9,8},{10,11... | collective-permute-start | bytes 393224 | tf_op jit(solution)/shard_map/ppermute | solution.py:356
  62.7 1.0 %collective-permute-done.got_ref = f32[4,64,128]{2,1,0:T(8,128)S(1)} collective-permute-done((f32[4,64,128]{2,1,0:T(8,128)S(1)}, f32[4,64,128]{2,1,0:T(8,128)S(1)}, u32[]{:S(2)}, u32[]{:S(2)}) %collective-permute-start) | collective-permute-done | bytes 131104 | tf_op jit(solution)/shard_map/ppermute | solution.py:356
  63.7 4.3 %collective-permute-start.1 = (f32[2,64,128]{2,1,0:T(8,128)S(1)}, f32[2,64,128]{2,1,0:T(8,128)S(1)}, u32[]{:S(2)}, u32[]{:S(2)}) collective-permute-start(f32[2,64,128]{2,1,0:T(8,128)S(1)} %slice_add_fusion.ga_ref), channel_id=1, source_target_pairs={{0,2},{2,0},{1,3},{3,1},{4,6},{6,4},{5,7},{7,5},{8,10},{10,8},{9,1... | collective-permute-start | bytes 196616 | tf_op jit(solution)/shard_map/ppermute | solution.py:358
  68.0 0.9 %prep.1 = (bf16[4,128,768]{2,1,0:T(8,128)(2,1)S(1)}, bf16[4,128,768]{2,1,0:T(8,128)(2,1)S(1)}, f32[4,64,128]{2,1,0:T(8,128)S(1)}, f32[4,128,768]{2,1,0:T(8,128)S(1)}) custom-call(f32[3200,128]{1,0:T(8,128)S(1)} %bitcast.5, f32[4,64,128]{2,1,0:T(8,128)S(1)} %gram.1.own_ref, f32[4,64,128]{2,1,0:T(8,128)S(1)} %collective-permute-done.got_ref), custom_call_target="tpu_custom_call" | custom-call | flops 10000000 | bytes 4000000 | tf_op jit(solution)/shard_map/prep/pallas_call | solution.py:261
  68.9 1.9 %collective-permute-done.1.gb_ref = f32[2,64,128]{2,1,0:T(8,128)S(1)} collective-permute-done((f32[2,64,128]{2,1,0:T(8,128)S(1)}, f32[2,64,128]{2,1,0:T(8,128)S(1)}, u32[]{:S(2)}, u32[]{:S(2)}) %collective-permute-start.1) | collective-permute-done | bytes 65568 | tf_op jit(solution)/shard_map/ppermute | solution.py:358
  70.8 1.9 %solve.1 = f32[4,2,64,768]{3,2,1,0:T(8,128)} custom-call(bf16[4,128,768]{2,1,0:T(8,128)(2,1)S(1)} %get-tuple-element.9.high_ref, bf16[4,128,768]{2,1,0:T(8,128)(2,1)S(1)} %get-tuple-element.10.low_ref, f32[4,64,128]{2,1,0:T(8,128)S(1)} %get-tuple-element.11.start_ref, f32[4,128,768]{2,1,0:T(8,128)S(1)} %get-tuple-element.12.rhs_ref, ...), custom_call_target="tpu_custom_call" | custom-call | flops 300000000 | bytes 4000000 | tf_op jit(solution)/shard_map/solve/pallas_call | solution.py:340
  (1 shorter events, 0.0 us)
Async XLA Ops:
  60.3 3.4 %collective-permute-start = (f32[4,64,128]{2,1,0:T(8,128)S(1)}, f32[4,64,128]{2,1,0:T(8,128)S(1)}, u32[]{:S(2)}, u32[]{:S(2)}) collective-permute-start(f32[4,64,128]{2,1,0:T(8,128)S(1)} %gram.1.own_ref), channel_id=1, source_target_pairs={{0,1},{1,0},{2,3},{3,2},{4,5},{5,4},{6,7},{7,6},{8,9},{9,8},{10,11... | collective-permute-start | bytes 393224 | tf_op jit(solution)/shard_map/ppermute | solution.py:356
  63.7 7.1 %collective-permute-start.1 = (f32[2,64,128]{2,1,0:T(8,128)S(1)}, f32[2,64,128]{2,1,0:T(8,128)S(1)}, u32[]{:S(2)}, u32[]{:S(2)}) collective-permute-start(f32[2,64,128]{2,1,0:T(8,128)S(1)} %slice_add_fusion.ga_ref), channel_id=1, source_target_pairs={{0,2},{2,0},{1,3},{3,1},{4,6},{6,4},{5,7},{7,5},{8,10},{10,8},{9,1... | collective-permute-start | bytes 196616 | tf_op jit(solution)/shard_map/ppermute | solution.py:358
